TPU v7x, 512 devices: a whole 4x4x16 slice. The times are simulated.
512 devices in a mesh: dp: 16 (over z), fsdp: 32 (over x, y, core).
Axes of the slice: x: 4, y: 4, z: 16, core: 2. Of those that a mesh axis runs over, the one named last changes fastest.
Arguments:
- txt_tokens: bfloat16 [512, 8, 3072], P(('dp', 'fsdp')), may hold values from -6 to 6
- concept_table: bfloat16 [4096, 3072], P('dp'), may hold values from -6 to 6
- concept_ids: int32 [512], P(('dp', 'fsdp')), may hold values from 0 to 4095
- positions: int32 [512], P(('dp', 'fsdp')), may hold values from 0 to 7
- timesteps: int32 [512], P(('dp', 'fsdp')), may hold values from 0 to 63
- counts: int32 [4096], P('dp'), may hold values from 1 to 16
- mod_table: bfloat16 [64, 2, 3072], P(None, None, 'fsdp'), may hold values from -1.5 to 1.5
- kv_weight: bfloat16 [3072, 3072], P('fsdp'), may hold values from -0.109375 to 0.109375
- kv_bias: float32 [3072], replicated, may hold values from -3 to 3
- key_gain: float32 [128], replicated, may hold values from 0.5 to 1.5
- img_query: bfloat16 [512, 192, 1536], P(('dp', 'fsdp')), may hold values from -256 to 256
- img_key: bfloat16 [512, 192, 1536], P(('dp', 'fsdp')), may hold values from -6 to 6
- img_value: bfloat16 [512, 192, 1536], P(('dp', 'fsdp')), may hold values from -6 to 6
- out_grad: bfloat16 [512, 192, 1536], P(('dp', 'fsdp')), may hold values from -6 to 6
Outputs:
- table_grad: float32 [4096, 3072], P('dp', 'fsdp')
Inputs may be any that keep to these rules, and one draw needn't show every extreme that they name: `concept_ids`: concept of each sample, some concepts far more common than others.
All inputs are finite; a program needn't handle non-finite values.
Results may differ from a plain program's by a relative error of at most 0.0083.
Values may be sent and summed in bfloat16 or wider, within the bound.
A program may use at most 64 MiB of HBM per device.

v0:
```python
import jax
import jax.numpy as jnp
from jax import lax
from jax.sharding import PartitionSpec as P

EPSILON = 1e-06


def layer_norm(values):
    centre = jnp.mean(values, -1, keepdims=True)
    spread = jnp.mean((values - centre) ** 2, -1, keepdims=True)
    inverse = lax.rsqrt(spread + EPSILON)
    return ((values - centre) * inverse, inverse[..., 0])


def shards(
    txt_tokens,
    concept_table,
    concept_ids,
    positions,
    timesteps,
    counts,
    mod_table,
    kv_weight,
    kv_bias,
    key_gain,
    img_query,
    img_key,
    img_value,
    out_grad,
):
    highest = lax.Precision.HIGHEST
    fsdp_size = lax.axis_size("fsdp")
    column = lax.axis_index("fsdp")
    tok_len = txt_tokens.shape[1]
    model_width = txt_tokens.shape[2]
    slice_width = kv_weight.shape[0]
    kv_width = kv_weight.shape[1]
    head_width = kv_width // 2
    head_dim = key_gain.shape[0]
    head_count = head_width // head_dim
    img_len = img_query.shape[1]
    bucket_count = mod_table.shape[0]
    root_dh = jnp.sqrt(jnp.float32(head_dim))
    table_hat, table_rstd = layer_norm(concept_table.astype(jnp.float32))
    table_part = lax.dynamic_slice_in_dim(
        table_hat.astype(jnp.bfloat16), column * slice_width, slice_width, 1
    )
    table_all = lax.all_gather(table_part, "dp", axis=0, tiled=True)
    own_hat = layer_norm(txt_tokens[0].astype(jnp.float32))[0].astype(jnp.bfloat16)
    labels = jnp.stack([concept_ids[0], positions[0], timesteps[0]])
    label_tile = jnp.tile(labels[None, :], (1, fsdp_size))
    token_cols, label_cols = (
        lax.all_to_all(own_hat, "fsdp", split_axis=1, concat_axis=0, tiled=True),
        lax.all_to_all(label_tile, "fsdp", split_axis=1, concat_axis=0, tiled=True),
    )
    group_ids = label_cols[:, 0]
    group_pos = label_cols[:, 1]
    group_time = label_cols[:, 2]
    concept_cols = jnp.take(table_all, group_ids, axis=0)
    token_cols = token_cols.reshape(fsdp_size, tok_len, slice_width)
    is_place = jnp.arange(tok_len, dtype=jnp.int32)[None, :] == group_pos[:, None]
    token_cols = jnp.where(is_place[:, :, None], concept_cols[:, None, :], token_cols)
    pick_time = (jnp.arange(bucket_count, dtype=jnp.int32)[None, :] == group_time[:, None]).astype(
        jnp.bfloat16
    )
    modulation = jnp.dot(
        pick_time,
        mod_table.reshape(bucket_count, 2 * slice_width),
        preferred_element_type=jnp.float32,
    )
    modulation = modulation.reshape(fsdp_size, 2, slice_width)
    shift_cols = modulation[:, 0]
    scale_cols = 1.0 + modulation[:, 1]
    modulated = (
        scale_cols[:, None, :] * token_cols.astype(jnp.float32) + shift_cols[:, None, :]
    ).astype(jnp.bfloat16)
    kv_terms = jnp.dot(
        modulated.reshape(fsdp_size * tok_len, slice_width),
        kv_weight,
        preferred_element_type=jnp.float32,
    )
    kv_terms = kv_terms.reshape(fsdp_size, tok_len, kv_width)
    weight_f = kv_weight.astype(jnp.float32)
    concept_f = concept_cols.astype(jnp.float32)
    side_rows = jnp.stack([scale_cols, scale_cols * concept_f], 1).reshape(
        fsdp_size * 2, slice_width
    )
    side_terms = jnp.dot(side_rows, weight_f, precision=highest).reshape(fsdp_size, 2, kv_width)
    all_terms = jnp.concatenate([kv_terms, side_terms], 1)
    row_block = all_terms.shape[1]
    all_terms = all_terms.reshape(fsdp_size * row_block, kv_width)
    own_rows = lax.psum_scatter(all_terms, "fsdp", scatter_dimension=0, tiled=True)
    kv_rows = own_rows[:tok_len] + kv_bias
    pos_pick = (jnp.arange(tok_len, dtype=jnp.int32) == positions[0]).astype(jnp.float32)
    key_raw = kv_rows[:, :head_width].reshape(tok_len, head_count, head_dim)
    key_inv = lax.rsqrt(jnp.mean(key_raw * key_raw, -1) + EPSILON)
    key_norm = (
        (key_raw * key_inv[..., None] * key_gain).astype(jnp.bfloat16).reshape(tok_len, head_width)
    )
    val_txt = kv_rows[:, head_width:].astype(jnp.bfloat16)
    keys_all = jnp.concatenate([key_norm, img_key[0]], 0).reshape(
        tok_len + img_len, head_count, head_dim
    )
    vals_all = jnp.concatenate([val_txt, img_value[0]], 0).reshape(
        tok_len + img_len, head_count, head_dim
    )
    queries = img_query[0].reshape(img_len, head_count, head_dim)
    scores = (
        jnp.einsum("qhd,khd->hqk", queries, keys_all, preferred_element_type=jnp.float32) / root_dh
    )
    row_top = jnp.max(scores, -1, keepdims=True)
    raised = jnp.exp(scores - row_top)
    prob_full = raised / jnp.sum(raised, -1, keepdims=True)
    prob_low = prob_full.astype(jnp.bfloat16)
    attended = jnp.einsum("hqk,khd->qhd", prob_low, vals_all, preferred_element_type=jnp.float32)
    grad_f = out_grad[0].reshape(img_len, head_count, head_dim).astype(jnp.float32)
    row_delta = jnp.einsum("qhd,qhd->hq", grad_f, attended)
    prob_pos = jnp.einsum("hqk,k->hq", prob_full[:, :, :tok_len], pos_pick, precision=highest)
    val_local = val_txt.reshape(tok_len, head_count, head_dim).astype(jnp.float32)
    val_pos = jnp.einsum("k,khd->hd", pos_pick, val_local, precision=highest)
    grad_prob = jnp.einsum("qhd,hd->hq", grad_f, val_pos, precision=highest)
    grad_score = prob_pos * (grad_prob - row_delta)
    grad_val = jnp.einsum("hq,qhd->hd", prob_pos, grad_f, precision=highest)
    grad_key = (
        jnp.einsum("hq,qhd->hd", grad_score, queries.astype(jnp.float32), precision=highest)
        / root_dh
    )
    raw_pos = jnp.einsum("k,khd->hd", pos_pick, key_raw, precision=highest)
    inv_pos = jnp.einsum("k,kh->h", pos_pick, key_inv, precision=highest)
    normed_key = raw_pos * inv_pos[:, None]
    grad_norm = grad_key * key_gain
    grad_raw = inv_pos[:, None] * (
        grad_norm - normed_key * jnp.mean(grad_norm * normed_key, -1, keepdims=True)
    )
    grad_kv = jnp.concatenate([grad_raw.reshape(head_width), grad_val.reshape(head_width)])[None, :]
    side_mean = (
        jnp.stack(
            [
                jnp.dot(grad_kv[0], own_rows[tok_len], precision=highest),
                jnp.dot(grad_kv[0], own_rows[tok_len + 1], precision=highest),
            ]
        )
        / model_width
    )
    grads_all, sides_all = (
        lax.all_gather(grad_kv, "fsdp", axis=0, tiled=True),
        lax.all_gather(side_mean[None, :], "fsdp", axis=0, tiled=True),
    )
    grad_cols = jnp.dot(grads_all, weight_f.T, precision=highest) * scale_cols
    row_grad = grad_cols - sides_all[:, 0:1] - concept_f * sides_all[:, 1:2]
    owner_scale = table_rstd / counts.astype(jnp.float32)
    conc_total = table_all.shape[0]
    one_hot = (jnp.arange(conc_total, dtype=jnp.int32)[:, None] == group_ids[None, :]).astype(
        jnp.float32
    )
    dense_rows = jnp.dot(one_hot, row_grad, precision=highest)
    owned_rows = lax.psum_scatter(dense_rows, "dp", scatter_dimension=0, tiled=True)
    return owned_rows * owner_scale[:, None]


def solution(mesh):
    placed = (
        P(("dp", "fsdp"), None, None),
        P("dp", None),
        P(("dp", "fsdp")),
        P(("dp", "fsdp")),
        P(("dp", "fsdp")),
        P("dp"),
        P(None, None, "fsdp"),
        P("fsdp", None),
        P(),
        P(),
        P(("dp", "fsdp"), None, None),
        P(("dp", "fsdp"), None, None),
        P(("dp", "fsdp"), None, None),
        P(("dp", "fsdp"), None, None),
    )
    return jax.shard_map(
        shards, mesh=mesh, in_specs=placed, out_specs=P("dp", "fsdp"), check_vma=False
    )
```

profile of v0, /device:TPU:2, one launch (start us, length us, event | category | flops | bytes accessed | tf_op | source)
XLA Modules:
  0.0 369.3 jit_solution(15416597220606547347)
XLA Ops:
  8.6 0.1 pad_add_fusion
  8.7 0.6 tile.2
  9.3 9.3 %all-to-all-start = ((s32[1,32,3]{2,0,1:T(1,128)}), s32[1,32,3]{2,0,1:T(1,128)S(1)}, u32[]{:S(2)}, u32[]{:S(2)}) async-start(s32[1,32,3]{2,0,1:T(1,128)} %tile.2), calls=%async_computation | async-start | bytes 32768 | tf_op jit(solution)/shard_map/all_to_all | solution.py:55
  18.6 0.9 convert_reduce_fusion.1
  19.6 0.9 reshape.234
  20.5 1.7 convert_reduce_fusion
  22.3 2.1 multiply_reduce_fusion
  24.4 0.6 convert_divide_fusion
  25.0 1.1 fusion.32
  26.1 39.8 %all_gather.9 = bf16[4096,96]{1,0:T(8,128)(2,1)S(1)} all-gather(bf16[256,96]{1,0:T(8,128)(2,1)S(1)} %fusion.32), channel_id=1, replica_groups=mesh['dp'=16,'fsdp'=32] {'dp'}, dimensions={0}, use_global_device_ids=true | all-gather | bytes 835584 | tf_op jit(solution)/shard_map/all_gather | solution.py:49
  65.9 0.2 fusion.36
  66.2 0.7 fusion.34
  66.9 0.1 reshape.228
  67.0 0.1 dot_general.56
  67.1 7.4 %all-to-all-start.1 = ((bf16[8,32,96]{2,0,1:T(8,128)(2,1)}), bf16[8,32,96]{2,0,1:T(8,128)(2,1)S(1)}, u32[]{:S(2)}, u32[]{:S(2)}) async-start(bf16[8,32,96]{2,0,1:T(8,128)(2,1)} %fusion.34), calls=%async_computation.1 | async-start | bytes 131072 | tf_op jit(solution)/shard_map/all_to_all | solution.py:54
  74.5 0.1 copy.35
  74.6 0.6 slice_bitcast_fusion.5
  75.2 0.6 gather_fusion
  75.8 0.2 fusion.47
  76.2 0.5 copy-done.11
  76.6 0.5 fusion.19
  77.2 0.6 copy.38
  77.8 3.0 all-to-all-done.1
  80.8 0.6 fusion.21
  81.4 3.4 pad_maximum_fusion
  84.8 5.3 %reshape.229 = f32[320,3072]{1,0:T(8,128)} reshape(f32[32,10,3072]{2,1,0:T(8,128)} %pad_maximum_fusion) | data formatting | bytes 7864320 | tf_op jit(solution)/shard_map/reshape | solution.py:92
  90.2 1.0 copy-done.7
  91.2 0.4 reshape_squeeze.6
  91.6 0.4 concatenate.29
  92.0 0.2 copy.39
  92.2 0.4 concatenate.31
  92.6 0.2 copy.41
  92.8 2.2 reshape_squeeze.7
  95.0 1.3 dynamic-slice
  97.0 0.5 broadcast_multiply_fusion.3
  97.4 126.6 %all-reduce.3.cloned.1.call-done = f32[320,3072]{1,0:T(8,128)} async-done(((f32[320,3072]{1,0:T(8,128)}), f32[320,3072]{1,0:T(8,128)}) %all-reduce.3.cloned.1.call-update) | async-done | bytes 3932176
  224.0 0.9 dynamic-slice_add_fusion
  225.0 0.1 fusion.42
  225.1 0.1 fusion.50
  225.2 0.5 fusion.12
  225.7 2.5 fusion.79
  228.2 0.4 broadcast_divide_fusion
  228.6 0.5 convolution_bitcast_fusion
  229.1 0.6 copy-done.2
  229.8 0.9 multiply_reduce_fusion.1
  230.6 0.1 copy.53
  230.7 1.0 fusion.6
  231.7 0.1 convolution_bitcast_fusion.1
  231.9 2.1 fusion.26
  234.0 1.7 fusion.28
  235.7 0.1 convolution_bitcast_fusion.2
  235.9 0.2 convolution_reduce_fusion
  236.1 0.2 fusion.60
  236.3 0.1 fusion.62
  236.3 0.6 fusion.24
  236.9 1.0 constant_dynamic-slice_fusion.1
  237.9 0.7 multiply_reduce_fusion.3
  238.6 1.4 fusion.68
  240.0 20.8 %all-gather.1 = f32[32,1,2]{2,1,0:T(1,128)S(1)} all-gather(f32[1,1,2]{2,1,0:T(1,128)S(1)} %fusion.68), channel_id=1, replica_groups=mesh['dp'=16,'fsdp'=32] {'fsdp'}, dimensions={0}, use_global_device_ids=true | all-gather | bytes 264 | tf_op jit(solution)/shard_map/all_gather | solution.py:148
  260.9 24.3 %all-gather = f32[98304]{0:T(1024)S(1)} all-gather(f32[3072]{0:T(1024)S(1)} %get-tuple-element.7), channel_id=2, replica_groups=mesh['dp'=16,'fsdp'=32] {'fsdp'}, dimensions={0}, use_global_device_ids=true | all-gather | bytes 405504 | tf_op jit(solution)/shard_map/all_gather | solution.py:147
  285.2 0.7 fusion.11
  285.9 2.0 fusion.23
  287.9 73.0 %reduce-scatter.2.cloned.1.call-done = f32[256,96]{0,1:T(8,128)} async-done(((f32[4096,96]{0,1:T(8,128)}), f32[256,96]{0,1:T(8,128)}) %reduce-scatter.2.cloned.1.call-update) | async-done | bytes 98320 | tf_op jit(solution)/shard_map/reduce_scatter | solution.py:158
  360.9 1.5 broadcast_multiply_fusion
  (60 shorter events, 0.7 us)
Async XLA Ops:
  6.5 70.1 %copy-start = (bf16[96,3072]{1,0:T(8,128)(2,1)S(1)}, bf16[96,3072]{1,0:T(8,128)(2,1)}, u32[]{:S(2)}) copy-start(bf16[96,3072]{1,0:T(8,128)(2,1)} %param.21) | copy-start | bytes 1769476
  6.5 15.7 %copy-start.1 = (bf16[256,3072]{1,0:T(8,128)(2,1)S(1)}, bf16[256,3072]{1,0:T(8,128)(2,1)}, u32[]{:S(2)}) copy-start(bf16[256,3072]{1,0:T(8,128)(2,1)} %param.15) | copy-start | bytes 4718596
  9.3 57.8 %all-to-all-start = ((s32[1,32,3]{2,0,1:T(1,128)}), s32[1,32,3]{2,0,1:T(1,128)S(1)}, u32[]{:S(2)}, u32[]{:S(2)}) async-start(s32[1,32,3]{2,0,1:T(1,128)} %tile.2), calls=%async_computation | async-start | bytes 32768 | tf_op jit(solution)/shard_map/all_to_all | solution.py:55
  22.2 2.2 copy-start.18
  22.2 43.7 %copy-start.10 = (bf16[1,8,3072]{2,1,0:T(8,128)(2,1)S(1)}, bf16[1,8,3072]{2,1,0:T(8,128)(2,1)}, u32[]{:S(2)}) copy-start(bf16[1,8,3072]{2,1,0:T(8,128)(2,1)} %param.14) | copy-start | bytes 147460
  22.3 44.6 %copy-start.13 = (bf16[64,2,96]{2,1,0:T(2,128)(2,1)S(1)}, bf16[64,2,96]{2,1,0:T(2,128)(2,1)}, u32[]{:S(2)}) copy-start(bf16[64,2,96]{2,1,0:T(2,128)(2,1)} %param.20) | copy-start | bytes 73732
  67.1 13.7 %all-to-all-start.1 = ((bf16[8,32,96]{2,0,1:T(8,128)(2,1)}), bf16[8,32,96]{2,0,1:T(8,128)(2,1)S(1)}, u32[]{:S(2)}, u32[]{:S(2)}) async-start(bf16[8,32,96]{2,0,1:T(8,128)(2,1)} %fusion.34), calls=%async_computation.1 | async-start | bytes 131072 | tf_op jit(solution)/shard_map/all_to_all | solution.py:54
  74.5 149.5 %all-reduce.3.cloned.1.call-start = ((), (), s32[]{:S(2)}) async-start(), calls=%async_computation.4 | async-start | bytes 7864320
  76.0 0.6 copy-start.11
  90.1 1.1 copy-start.7
  90.1 1.5 copy-start.8
  90.1 2.1 copy-start.9
  90.1 270.8 %reduce-scatter.2.cloned.1.call-start = ((), (), s32[]{:S(2)}) async-start(), calls=%async_computation.3 | async-start | bytes 1671168 | tf_op jit(solution)/shard_map/reduce_scatter | solution.py:158
  91.6 133.6 %copy-start.4 = (bf16[192,12,128]{2,1,0:T(8,128)(2,1)}, bf16[192,12,128]{2,1,0:T(8,128)(2,1)S(1)}, u32[]{:S(2)}) copy-start(bf16[192,12,128]{2,1,0:T(8,128)(2,1)S(1)} %reshape_squeeze.6) | copy-start | bytes 1769476
  92.2 4.8 %copy-start.19 = (f32[128]{0:T(128)S(1)}, f32[128]{0:T(128)}, u32[]{:S(2)}) copy-start(f32[128]{0:T(128)} %param.23) | copy-start | bytes 1540
  92.6 131.4 %copy-start.14 = (f32[3072]{0:T(1024)S(1)}, f32[3072]{0:T(1024)}, u32[]{:S(2)}) copy-start(f32[3072]{0:T(1024)} %param.22) | copy-start | bytes 36868
  225.0 3.2 copy-start.5
  228.6 1.1 copy-start.2
  229.7 2.0 copy-start.6
  229.8 6.3 %copy-start.17 = (f32[128]{0:T(128)S(1)}, f32[128]{0:T(128)}, u32[]{:S(2)}) copy-start(f32[128]{0:T(128)} %broadcast_multiply_fusion.3) | copy-start | bytes 1540
  230.7 5.7 %copy-start.3 = (bf16[192,12,128]{2,1,0:T(8,128)(2,1)S(1)}, bf16[192,12,128]{2,1,0:T(8,128)(2,1)}, u32[]{:S(2)}) copy-start(bf16[192,12,128]{2,1,0:T(8,128)(2,1)} %reshape_squeeze.7) | copy-start | bytes 1769476
  230.7 54.6 %copy-start.12 = (f32[32,2,96]{2,0,1:T(8,128)S(1)}, f32[32,2,96]{2,0,1:T(8,128)}, u32[]{:S(2)}) copy-start(f32[32,2,96]{2,0,1:T(8,128)} %copy-done.11) | copy-start | bytes 73732
  231.7 54.2 %copy-start.16 = (s32[32]{0:T(128)S(1)}, s32[32]{0:T(128)}, u32[]{:S(2)}) copy-start(s32[32]{0:T(128)} %get-tuple-element.16) | copy-start | bytes 388
  285.2 75.7 %copy-start.15 = (f32[256]{0:T(256)S(1)}, f32[256]{0:T(256)}, u32[]{:S(2)}) copy-start(f32[256]{0:T(256)} %get-tuple-element.20) | copy-start | bytes 3076
Sparse Core Ops, SparseCore 0:
  90.2 133.7 all-reduce.2
  288.1 72.8 reduce-scatter.1
where the time goes:
time: 370 us; the launch traced here: 369 us
  waiting for transfers between devices  203 us (55%)
  blocking collectives  84.9 us (23%)
  other arithmetic  21 us (6%)
  starting transfers between devices  16.8 us (5%)
  local copies, waits for them, and re-layouts  16.7 us (5%)
  between operations  16.5 us (4%)
  matrix products  10.8 us (3%)
    unnamed x3, waiting for transfers between devices  127 us
    reduce_scatter x1, waiting for transfers between devices, shards(): lax.psum_scatter(dense_rows, 'dp', scatter_dimension=0, tiled=True)  73 us
    all_gather x1, blocking collectives, shards(): table_all = lax.all_gather(table_part, 'dp', axis=0, tiled=True)  39.8 us
    all_gather x1, blocking collectives, shards(): lax.all_gather(grad_kv, 'fsdp', axis=0, tiled=True)  24.3 us
    all_gather x1, blocking collectives, shards(): lax.all_gather(side_mean[None, :], 'fsdp', axis=0, tiled=True)  20.8 us
    all_to_all x1, starting transfers between devices, shards(): lax.all_to_all(label_tile, 'fsdp', split_axis=1, concat_axis=0, tiled=True)  9.32 us
  transfers between devices with their start and end apart: 4, of which 3 were waited for; matrix products, arithmetic and copies ran while one was open for 5% of the time, Pallas kernels for 0%

commit v1 on v0

v1 whole, which is shorter than its diff:
```python
import functools
import jax
import jax.numpy as jnp
from jax import lax
from jax.experimental import pallas as pl
from jax.experimental.pallas import tpu as pltpu
from jax.sharding import PartitionSpec as P

EPSILON = 1e-06
LANES = 128
BF = jnp.bfloat16
F32 = jnp.float32
MESH = pl.DeviceIdType.MESH
NT_DIMS = (((1,), (1,)), ((), ()))
TN_DIMS = (((0,), (0,)), ((), ()))


def split_two(values):
    high = values.astype(BF)
    low = (values - high.astype(F32)).astype(BF)
    return high, low


def iota(shape, axis):
    return lax.broadcasted_iota(jnp.int32, shape, axis)


def step_kernel(
    dims,
    ids_s,
    pos_s,
    time_s,
    tok,
    table,
    counts,
    modp,
    weight,
    bias,
    gain,
    q_any,
    k_any,
    v_any,
    g_any,
    out,
    q,
    k,
    v,
    g,
    id_buf,
    id_own,
    row32,
    row_send,
    row_recv,
    c32,
    c_row,
    tok_msg,
    tok_recv,
    w_recv,
    mod_recv,
    mod_all,
    part,
    part_recv,
    side,
    side_recv,
    kv,
    m_img,
    l_img,
    d_img,
    dkv32,
    raw32,
    s1_32,
    s2_32,
    dkv_own,
    dkv_recv,
    dkv_wide,
    g_own,
    g_recv,
    load_sem,
    send_sem,
    recv_sem,
):
    zs, ns, m = dims
    z = lax.axis_index("dp")
    f = lax.axis_index("fsdp")
    groups = ns // m
    r = lax.rem(f, m)
    grp = lax.div(f, m)
    tok_len, width = tok.shape
    slice_w = weight.shape[0]
    kv_w = weight.shape[1]
    head_w = kv_w // 2
    heads = head_w // LANES
    block = kv_w // m
    group_w = slice_w * m
    n_img = q.shape[0]
    rows_own = table.shape[0]
    buckets = modp.shape[0] // 2
    inv_root = 1.0 / (LANES**0.5)

    loads = [
        pltpu.make_async_copy(src, dst, load_sem.at[i])
        for i, (src, dst) in enumerate(((q_any, q), (k_any, k), (v_any, v), (g_any, g)))
    ]
    for copy in loads:
        copy.start()

    barrier = pltpu.get_barrier_semaphore()

    def greet_plane(j, c):
        pl.semaphore_signal(
            barrier, inc=1, device_id=(z, lax.rem(f + j, ns)), device_id_type=MESH
        )
        return c

    def greet_line(j, c):
        pl.semaphore_signal(
            barrier, inc=1, device_id=(lax.rem(z + j, zs), f), device_id_type=MESH
        )
        return c

    lax.fori_loop(1, zs, greet_line, 0)
    lax.fori_loop(1, ns, greet_plane, 0)

    own_id = ids_s[0]
    own_pos = pos_s[0]
    own_time = time_s[0]
    id_own[...] = jnp.full(id_own.shape, own_id, jnp.int32)
    id_buf[z] = id_own[...]
    w_recv[pl.ds(pl.multiple_of(r * slice_w, 16), slice_w), :] = weight[
        :, pl.ds(pl.multiple_of(r * block, LANES), block)
    ]
    mod_recv[r] = modp[...]

    pl.semaphore_wait(barrier, zs - 1 + ns - 1)

    def remote(src, dst, phase, device):
        return pltpu.make_async_remote_copy(
            src_ref=src,
            dst_ref=dst,
            send_sem=send_sem.at[phase],
            recv_sem=recv_sem.at[phase],
            device_id=device,
            device_id_type=MESH,
        )

    def finish(ref, phase):
        pltpu.make_async_copy(ref, ref, recv_sem.at[phase]).wait()

    def drain(ref, phase):
        pltpu.make_async_copy(ref, ref, send_sem.at[phase]).wait()

    def send_id(j, c):
        remote(id_own, id_buf.at[z], 0, (lax.rem(z + j, zs), f)).start()
        return c

    lax.fori_loop(1, zs, send_id, 0)

    def send_weight(j, c):
        peer = lax.rem(r + j, m)
        device = (z, grp * m + peer)
        remote(
            weight.at[:, pl.ds(pl.multiple_of(peer * block, LANES), block)],
            w_recv.at[pl.ds(pl.multiple_of(r * slice_w, 16), slice_w), :],
            1,
            device,
        ).start()
        remote(modp, mod_recv.at[r], 2, device).start()
        return c

    lax.fori_loop(1, m, send_weight, 0)

    for copy in loads:
        copy.wait()

    def image_head(h, c):
        lanes = pl.ds(pl.multiple_of(h * LANES, LANES), LANES)
        scores = (
            lax.dot_general(k[:, lanes], q[:, lanes], NT_DIMS, preferred_element_type=F32)
            * inv_root
        )
        grads = lax.dot_general(v[:, lanes], g[:, lanes], NT_DIMS, preferred_element_type=F32)
        top = jnp.max(scores, 0, keepdims=True)
        raised = jnp.exp(scores - top)
        m_img[h] = top
        l_img[h] = jnp.sum(raised, 0, keepdims=True)
        d_img[h] = jnp.sum(raised.astype(BF).astype(F32) * grads, 0, keepdims=True)
        return c

    half = heads // 2
    lax.fori_loop(0, half, image_head, 0)

    tok_f = tok[...].astype(F32)
    centre = jnp.mean(tok_f, -1, keepdims=True)
    spread = jnp.mean((tok_f - centre) ** 2, -1, keepdims=True)
    tok_hat = ((tok_f - centre) * lax.rsqrt(spread + EPSILON)).astype(BF).astype(F32)

    finish(id_buf.at[pl.ds(0, zs - 1)], 0)
    wanted = id_buf[:, 0, :][:, :1]
    pick = (iota((zs, rows_own), 1) + z * rows_own == wanted).astype(F32).astype(BF)
    rows = jnp.dot(pick, table[...], preferred_element_type=F32)
    for c in range(width // LANES):
        row32[:, c, :] = rows[:, c * LANES : (c + 1) * LANES]
    row_send[...] = row32[...].astype(BF)
    row_recv[z] = row_send[z]

    def send_row(j, c):
        peer = lax.rem(z + j, zs)
        remote(row_send.at[peer], row_recv.at[z], 3, (peer, f)).start()
        return c

    lax.fori_loop(1, zs, send_row, 0)

    lax.fori_loop(half, heads, image_head, 0)

    finish(mod_recv.at[pl.ds(0, m - 1)], 2)
    lane_row = iota((LANES, group_w), 0)
    lane_col = iota((LANES, group_w), 1)
    mods = jnp.zeros((2 * buckets, group_w), F32)
    for c in range(m):
        place = ((lane_col == lane_row + c * slice_w) & (lane_row < slice_w)).astype(F32)
        mods += jnp.dot(mod_recv[c], place.astype(BF), preferred_element_type=F32)
    mod_all[...] = mods.astype(BF)

    table_f = table[...].astype(F32)
    t_centre = jnp.mean(table_f, -1, keepdims=True)
    t_spread = jnp.mean((table_f - t_centre) ** 2, -1, keepdims=True)
    t_rstd = lax.rsqrt(t_spread + EPSILON)
    diag = iota((rows_own, rows_own), 0) == iota((rows_own, rows_own), 1)
    count_col = jnp.sum(
        jnp.where(diag, counts[...].astype(F32), 0.0), -1, keepdims=True
    )
    own_scale = t_rstd / count_col

    finish(row_recv.at[pl.ds(0, zs - 1)], 3)
    concept = jnp.sum(row_recv[...].astype(F32), 0)
    c_mean = jnp.sum(jnp.sum(concept, -1, keepdims=True), 0, keepdims=True) / width
    c_diff = concept - c_mean
    c_var = jnp.sum(jnp.sum(c_diff * c_diff, -1, keepdims=True), 0, keepdims=True) / width
    c32[...] = c_diff * lax.rsqrt(c_var + EPSILON)
    for c in range(width // LANES):
        c_row[:, c * LANES : (c + 1) * LANES] = c32[c : c + 1, :]
    at_pos = iota((tok_len, 1), 0) == own_pos
    normed = jnp.where(at_pos, c_row[...], tok_hat).astype(BF)
    lab_lane = iota((tok_len, LANES), 1)
    lab_row = iota((tok_len, LANES), 0)
    id_high = lax.div(own_id, 64)
    id_low = lax.rem(own_id, 64)
    label = jnp.where(lab_lane == 0, own_time, 0)
    label = jnp.where((lab_lane == 1) & (lab_row == own_pos), 1, label)
    label = jnp.where(lab_lane == 2, id_high, label)
    label = jnp.where(lab_lane == 3, id_low, label)
    label = label.astype(F32).astype(BF)
    for c in range(groups):
        tok_msg[c, :, :group_w] = normed[:, c * group_w : (c + 1) * group_w]
        tok_msg[c, :, group_w:] = label
    tok_recv[f] = tok_msg[grp]

    def send_tok(j, c):
        peer = lax.rem(f + j, ns)
        remote(tok_msg.at[lax.div(peer, m)], tok_recv.at[f], 4, (z, peer)).start()
        return c

    lax.fori_loop(1, ns, send_tok, 0)
    finish(w_recv.at[pl.ds(0, (m - 1) * slice_w)], 1)
    finish(tok_recv.at[pl.ds(0, ns - 1)], 4)

    all_rows = tok_recv[...].astype(F32).reshape(ns * tok_len, group_w + LANES)
    toks = all_rows[:, :group_w]
    labels = all_rows[:, group_w:]
    times = labels[:, 0:1].astype(jnp.int32)
    placed = labels[:, 1:2]
    pick_time = (iota((ns * tok_len, buckets), 1) == times).astype(F32).astype(BF)
    shift = jnp.dot(pick_time, mod_all[:buckets, :], preferred_element_type=F32)
    scale = 1.0 + jnp.dot(pick_time, mod_all[buckets:, :], preferred_element_type=F32)
    modulated = (scale * toks + shift).astype(BF)
    terms = jnp.dot(modulated, w_recv[...], preferred_element_type=F32)
    part[...] = terms.reshape(ns, tok_len, block)
    concepts = jnp.sum((toks * placed).reshape(ns, tok_len, group_w), 1)
    scales = jnp.sum((scale * placed).reshape(ns, tok_len, group_w), 1)
    a_high, a_low = split_two(scales)
    b_high, b_low = split_two(scales * concepts)
    extra = jnp.dot(
        jnp.concatenate([a_high, a_low, b_high, b_low], 0),
        w_recv[...],
        preferred_element_type=F32,
    )
    side[:, 0, :] = extra[:ns] + extra[ns : 2 * ns]
    side[:, 1, :] = extra[2 * ns : 3 * ns] + extra[3 * ns :]
    part_recv[f] = part[f]
    side_recv[f] = side[f]

    def send_part(j, c):
        peer = lax.rem(f + j, ns)
        remote(part.at[peer], part_recv.at[f], 5, (z, peer)).start()
        remote(side.at[peer], side_recv.at[f], 6, (z, peer)).start()
        return c

    lax.fori_loop(1, ns, send_part, 0)

    labels_s = labels.reshape(ns, tok_len, LANES)[:, 0, :]
    pick_s = (
        (iota((ns, buckets), 1) == labels_s[:, 0:1].astype(jnp.int32)).astype(F32).astype(BF)
    )
    scale_own = 1.0 + jnp.dot(pick_s, modp[buckets:, :], preferred_element_type=F32)
    own_row = iota((group_w, LANES), 0)
    own_col = iota((group_w, LANES), 1)
    own_place = ((own_row == own_col + r * slice_w) & (own_col < slice_w)).astype(F32).astype(BF)
    concept_own = jnp.dot(concepts.astype(BF), own_place, preferred_element_type=F32)

    finish(part_recv.at[pl.ds(0, ns - 1)], 5)
    finish(side_recv.at[pl.ds(0, ns - 1)], 6)
    per = block // LANES
    for c in range(m):
        total = part_recv[c]
        extras = side_recv[c]
        for a in range(1, groups):
            total += part_recv[a * m + c]
            extras += side_recv[a * m + c]
        kv[:, c * block : (c + 1) * block] = total
        for b in range(per):
            s1_32[c * per + b : c * per + b + 1, :] = extras[0:1, b * LANES : (b + 1) * LANES]
            s2_32[c * per + b : c * per + b + 1, :] = extras[1:2, b * LANES : (b + 1) * LANES]

    kv_all = kv[...] + bias[...]
    pos_f = at_pos.astype(F32)
    gains = gain[...]
    raw_row = jnp.sum(kv_all[:, :head_w] * pos_f, 0, keepdims=True)
    key_parts = []
    for h in range(heads):
        raw = kv_all[:, h * LANES : (h + 1) * LANES]
        inv = lax.rsqrt(jnp.mean(raw * raw, -1, keepdims=True) + EPSILON)
        key_parts.append((raw * inv * gains).astype(BF).astype(F32))
        raw32[h : h + 1, :] = raw_row[:, h * LANES : (h + 1) * LANES]
    key_txt = jnp.concatenate(key_parts, 1)
    val_txt = kv_all[:, head_w:].astype(BF).astype(F32)
    own_head = iota((heads * tok_len, head_w), 0) // tok_len == iota(
        (heads * tok_len, head_w), 1
    ) // LANES
    key_diag = jnp.where(own_head, jnp.concatenate([key_txt] * heads, 0), 0.0).astype(BF)
    val_diag = jnp.where(own_head, jnp.concatenate([val_txt] * heads, 0), 0.0).astype(BF)
    s_txt = (
        lax.dot_general(key_diag, q[...], NT_DIMS, preferred_element_type=F32) * inv_root
    ).reshape(heads, tok_len, n_img)
    g_txt = lax.dot_general(val_diag, g[...], NT_DIMS, preferred_element_type=F32).reshape(
        heads, tok_len, n_img
    )
    top_img = m_img[...]
    top = jnp.maximum(top_img, jnp.max(s_txt, 1, keepdims=True))
    raised = jnp.exp(s_txt - top)
    alpha = jnp.exp(top_img - top)
    denom = alpha * l_img[...] + jnp.sum(raised, 1, keepdims=True)
    probs = raised / denom
    delta = alpha * d_img[...] / denom + jnp.sum(
        probs.astype(BF).astype(F32) * g_txt, 1, keepdims=True
    )
    pos_3 = (iota((1, tok_len, 1), 1) == own_pos).astype(F32)
    p_pos = jnp.sum(probs * pos_3, 1)
    g_pos = jnp.sum(g_txt * pos_3, 1)
    d_score = p_pos * (g_pos - delta[:, 0, :]) * inv_root
    p_high, p_low = split_two(p_pos)
    d_high, d_low = split_two(d_score)
    d_val = jnp.dot(
        jnp.concatenate([p_high.astype(F32), p_low.astype(F32)], 0).astype(BF),
        g[...],
        preferred_element_type=F32,
    )
    d_key = jnp.dot(
        jnp.concatenate([d_high.astype(F32), d_low.astype(F32)], 0).astype(BF),
        q[...],
        preferred_element_type=F32,
    )
    d_val = d_val[:heads] + d_val[heads:]
    d_key = d_key[:heads] + d_key[heads:]
    dkv32[...] = jnp.zeros(dkv32.shape, F32)
    for h in range(heads):
        dkv32[h : h + 1, :] = d_key[h : h + 1, h * LANES : (h + 1) * LANES]
        dkv32[heads + h : heads + h + 1, :] = d_val[h : h + 1, h * LANES : (h + 1) * LANES]
    raw_pos = raw32[...]
    inv_pos = lax.rsqrt(jnp.mean(raw_pos * raw_pos, -1, keepdims=True) + EPSILON)
    n_pos = raw_pos * inv_pos
    d_norm = dkv32[:heads, :] * gains
    dkv32[:heads, :] = inv_pos * (d_norm - n_pos * jnp.mean(d_norm * n_pos, -1, keepdims=True))
    dkv_rows = dkv32[: 2 * heads, :].astype(BF).astype(F32)
    mean_1 = jnp.sum(jnp.sum(dkv_rows * s1_32[...], -1, keepdims=True), 0, keepdims=True) / width
    mean_2 = jnp.sum(jnp.sum(dkv_rows * s2_32[...], -1, keepdims=True), 0, keepdims=True) / width
    for c, value in enumerate((mean_1, mean_2)):
        high, low = split_two(value)
        at = 2 * heads + 2 * c
        dkv32[at : at + 1, :] = jnp.broadcast_to(high.astype(F32), (1, LANES))
        dkv32[at + 1 : at + 2, :] = jnp.broadcast_to(low.astype(F32), (1, LANES))
    dkv_own[...] = dkv32[...].astype(BF)
    dkv_recv[f] = dkv_own[...]

    def send_dkv(j, c):
        remote(dkv_own, dkv_recv.at[f], 7, (z, lax.rem(f + j, ns))).start()
        return c

    lax.fori_loop(1, ns, send_dkv, 0)
    finish(dkv_recv.at[pl.ds(0, ns - 1)], 7)
    dkv_wide[...] = dkv_recv[...].astype(F32)
    grads = jnp.zeros((ns, slice_w), F32)
    for c in range(2 * heads):
        grads += lax.dot_general(
            dkv_wide[:, c, :].astype(BF),
            weight[:, c * LANES : (c + 1) * LANES],
            NT_DIMS,
            preferred_element_type=F32,
        )
    at = 2 * heads
    mean_1 = (dkv_wide[:, at, :] + dkv_wide[:, at + 1, :])[:, :slice_w]
    mean_2 = (dkv_wide[:, at + 2, :] + dkv_wide[:, at + 3, :])[:, :slice_w]
    row_grad = grads * scale_own[:, :slice_w] - mean_1 - concept_own[:, :slice_w] * mean_2
    g_own[:, :slice_w] = row_grad.astype(BF)
    g_own[:, slice_w:] = labels_s[:, : LANES - slice_w].astype(BF)
    g_recv[z] = g_own[...]

    def send_grad(j, c):
        remote(g_own, g_recv.at[z], 8, (lax.rem(z + j, zs), f)).start()
        return c

    lax.fori_loop(1, zs, send_grad, 0)
    finish(g_recv.at[pl.ds(0, zs - 1)], 8)
    every = g_recv[...].astype(F32).reshape(zs * ns, LANES)
    who = (every[:, slice_w + 2 : slice_w + 3] * 64.0 + every[:, slice_w + 3 : slice_w + 4]).astype(
        jnp.int32
    )
    belongs = (iota((zs * ns, rows_own), 1) + z * rows_own == who).astype(F32).astype(BF)
    summed = lax.dot_general(
        belongs, every.astype(BF), TN_DIMS, preferred_element_type=F32
    )
    out[...] = (summed * own_scale)[:, :slice_w]

    drain(id_buf.at[pl.ds(0, zs - 1)], 0)
    drain(w_recv.at[pl.ds(0, (m - 1) * slice_w)], 1)
    drain(mod_recv.at[pl.ds(0, m - 1)], 2)
    drain(row_recv.at[pl.ds(0, zs - 1)], 3)
    drain(tok_recv.at[pl.ds(0, ns - 1)], 4)
    drain(part_recv.at[pl.ds(0, ns - 1)], 5)
    drain(side_recv.at[pl.ds(0, ns - 1)], 6)
    drain(dkv_recv.at[pl.ds(0, ns - 1)], 7)
    drain(g_recv.at[pl.ds(0, zs - 1)], 8)


def shards(
    txt_tokens,
    concept_table,
    concept_ids,
    positions,
    timesteps,
    counts,
    mod_table,
    kv_weight,
    kv_bias,
    key_gain,
    img_query,
    img_key,
    img_value,
    out_grad,
):
    ns = lax.axis_size("fsdp")
    zs = lax.axis_size("dp")
    m = 8 if ns % 16 == 0 else 4
    tok_len, width = txt_tokens.shape[1:]
    slice_w, kv_w = kv_weight.shape
    head_w = kv_w // 2
    heads = head_w // LANES
    n_img = img_query.shape[1]
    buckets = mod_table.shape[0]
    rows_own = concept_table.shape[0]
    block = kv_w // m
    group_w = slice_w * m
    n_c = width // LANES
    slot = (2 * heads + 4 + 15) // 16 * 16

    modp = jnp.pad(
        mod_table.transpose(1, 0, 2).reshape(2 * buckets, slice_w), ((0, 0), (0, LANES - slice_w))
    )
    vm = pl.BlockSpec(memory_space=pltpu.VMEM)
    sm = pl.BlockSpec(memory_space=pltpu.SMEM)
    hb = pl.BlockSpec(memory_space=pl.ANY)
    image = pltpu.VMEM((n_img, head_w), BF)
    stat = pltpu.VMEM((heads, 1, n_img), F32)
    return pl.pallas_call(
        functools.partial(step_kernel, (zs, ns, m)),
        out_shape=jax.ShapeDtypeStruct((rows_own, slice_w), F32),
        in_specs=[sm] * 3 + [vm] * 7 + [hb] * 4,
        out_specs=vm,
        scratch_shapes=[
            image,
            image,
            image,
            image,
            pltpu.VMEM((zs, 1, LANES), jnp.int32),
            pltpu.VMEM((1, LANES), jnp.int32),
            pltpu.VMEM((zs, n_c, LANES), F32),
            pltpu.VMEM((zs, n_c, LANES), BF),
            pltpu.VMEM((zs, n_c, LANES), BF),
            pltpu.VMEM((n_c, LANES), F32),
            pltpu.VMEM((1, width), F32),
            pltpu.VMEM((ns // m, tok_len, group_w + LANES), BF),
            pltpu.VMEM((ns, tok_len, group_w + LANES), BF),
            pltpu.VMEM((group_w, block), BF),
            pltpu.VMEM((m, 2 * buckets, LANES), BF),
            pltpu.VMEM((2 * buckets, group_w), BF),
            pltpu.VMEM((ns, tok_len, block), F32),
            pltpu.VMEM((ns, tok_len, block), F32),
            pltpu.VMEM((ns, 2, block), F32),
            pltpu.VMEM((ns, 2, block), F32),
            pltpu.VMEM((tok_len, kv_w), F32),
            stat,
            stat,
            stat,
            pltpu.VMEM((slot, LANES), F32),
            pltpu.VMEM((heads, LANES), F32),
            pltpu.VMEM((2 * heads, LANES), F32),
            pltpu.VMEM((2 * heads, LANES), F32),
            pltpu.VMEM((slot, LANES), BF),
            pltpu.VMEM((ns, slot, LANES), BF),
            pltpu.VMEM((ns, slot, LANES), F32),
            pltpu.VMEM((ns, LANES), BF),
            pltpu.VMEM((zs, ns, LANES), BF),
            pltpu.SemaphoreType.DMA((4,)),
            pltpu.SemaphoreType.DMA((9,)),
            pltpu.SemaphoreType.DMA((9,)),
        ],
        compiler_params=pltpu.CompilerParams(collective_id=0, has_side_effects=True),
    )(
        concept_ids,
        positions,
        timesteps,
        txt_tokens[0],
        concept_table,
        counts[None, :],
        modp,
        kv_weight,
        kv_bias[None, :],
        key_gain[None, :],
        img_query[0],
        img_key[0],
        img_value[0],
        out_grad[0],
    )


def solution(mesh):
    placed = (
        P(("dp", "fsdp"), None, None),
        P("dp", None),
        P(("dp", "fsdp")),
        P(("dp", "fsdp")),
        P(("dp", "fsdp")),
        P("dp"),
        P(None, None, "fsdp"),
        P("fsdp", None),
        P(),
        P(),
        P(("dp", "fsdp"), None, None),
        P(("dp", "fsdp"), None, None),
        P(("dp", "fsdp"), None, None),
        P(("dp", "fsdp"), None, None),
    )
    return jax.shard_map(
        shards, mesh=mesh, in_specs=placed, out_specs=P("dp", "fsdp"), check_vma=False
    )
```

time: 370 us -> 75.9 us (0.21)
  the two profiles are of different devices: /device:TPU:2 before, /device:TPU:4 now
where the time goes in v1:
time: 75.9 us; the launch traced here: 75.6 us
  Pallas kernels  70.7 us (93%)
  local copies, waits for them, and re-layouts  3.03 us (4%)
  between operations  1.95 us (3%)
    pallas_call x1, Pallas kernels, shards(): pl.pallas_call(functools.partial(step_kernel, (zs, ns, m)), out_shape=jax...  70.7 us
    pallas_call x1, local copies, waits for them, and re-layouts, shards(): pl.pallas_call(functools.partial(step_kernel, (zs, ns, m)), out_shape=jax...  1.64 us

profile of v1, /device:TPU:4, one launch (start us, length us, event | category | flops | bytes accessed | tf_op | source)
XLA Modules:
  0.0 75.6 jit_solution(3149944527370022001)
XLA Ops:
  1.9 0.8 %copy.15 = bf16[2,64,96]{2,1,0:T(8,128)(2,1)S(1)} copy(bf16[2,64,96]{2,0,1:T(2,128)(2,1)} %bitcast.16) | data formatting | bytes 49152 | tf_op jit(solution)/shard_map/transpose | solution.py:476
  2.7 0.6 pad.4.modp
  3.3 70.7 %shard_map.136 = f32[256,96]{1,0:T(8,128)} custom-call(s32[1]{0:T(128)S(6)} %copy.17.ids_s, s32[1]{0:T(128)S(6)} %copy.18.pos_s, s32[1]{0:T(128)S(6)} %copy.19.time_s, bf16[8,3072]{1,0:T(8,128)(2,1)} %bitcast.15, bf16[256,3072]{1,0:T(8,128)(2,1)} %table.1, s32[1,256]{1,0:T(1,128)} %bitcast.18, bf16[128,128]{1,0:T(8,128)(2,1)} %pad.4.modp, ...), custom_call_target="tpu_custom_call" | custom-call | tf_op jit(solution)/shard_map/pallas_call | solution.py:483
  74.0 1.6 %copy.16 = f32[256,96]{0,1:T(8,128)} copy(f32[256,96]{1,0:T(8,128)} %shard_map.136) | data formatting | bytes 196608 | tf_op jit(solution)/shard_map/pallas_call | solution.py:483

commit v2 on v1

--- a/solution.py
+++ b/solution.py
@@ -25,27 +25,40 @@
     return lax.broadcasted_iota(jnp.int32, shape, axis)
 
 
+def far_first(sizes):
+    steps = [(a, b, c) for a in range(sizes[0]) for b in range(sizes[1]) for c in range(2)]
+
+    def hops(step):
+        return sum(min(d, n - d) for d, n in zip(step[:2], sizes))
+
+    return sorted(steps[1:], key=lambda step: (-hops(step), step))
+
+
 def step_kernel(
     dims,
     ids_s,
     pos_s,
     time_s,
     tok,
-    table,
     counts,
-    modp,
-    weight,
+    mods,
     bias,
     gain,
+    table_any,
+    weight_any,
     q_any,
     k_any,
     v_any,
     g_any,
     out,
+    table,
+    weight,
     q,
     k,
     v,
     g,
+    mod32,
+    modp,
     id_buf,
     id_own,
     row32,
@@ -55,13 +68,15 @@
     c_row,
     tok_msg,
     tok_recv,
+    c_msg,
+    c_recv,
     w_recv,
     mod_recv,
     mod_all,
     part,
     part_recv,
-    side,
-    side_recv,
+    late,
+    late_recv,
     kv,
     m_img,
     l_img,
@@ -79,10 +94,12 @@
     send_sem,
     recv_sem,
 ):
-    zs, ns, m = dims
+    zs, nx, ny = dims
+    ns = nx * ny * 2
+    m = ny * 2
     z = lax.axis_index("dp")
     f = lax.axis_index("fsdp")
-    groups = ns // m
+    groups = nx
     r = lax.rem(f, m)
     grp = lax.div(f, m)
     tok_len, width = tok.shape
@@ -94,42 +111,73 @@
     group_w = slice_w * m
     n_img = q.shape[0]
     rows_own = table.shape[0]
-    buckets = modp.shape[0] // 2
+    buckets = mods.shape[0]
     inv_root = 1.0 / (LANES**0.5)
 
+    my_y = lax.div(r, 2)
+    my_c = lax.rem(r, 2)
+    x_at = [lax.rem(grp + d, nx) for d in range(nx)]
+    y_at = [lax.rem(my_y + d, ny) * 2 for d in range(ny)]
+    c_at = [my_c, 1 - my_c]
+    plane = [(x_at[a], y_at[b] + c_at[c]) for a, b, c in far_first((nx, ny))]
+    mates = [y_at[b] + c_at[c] for a, b, c in far_first((nx, ny)) if a == 0]
+    line = [
+        lax.rem(z + d, zs) for d in sorted(range(1, zs), key=lambda d: (-min(d, zs - d), d))
+    ]
+
+    table_load = pltpu.make_async_copy(table_any, table, load_sem.at[0])
+    weight_load = pltpu.make_async_copy(weight_any, weight, load_sem.at[1])
     loads = [
-        pltpu.make_async_copy(src, dst, load_sem.at[i])
+        pltpu.make_async_copy(src, dst, load_sem.at[2 + i])
         for i, (src, dst) in enumerate(((q_any, q), (k_any, k), (v_any, v), (g_any, g)))
     ]
+    weight_load.start()
+    table_load.start()
     for copy in loads:
         copy.start()
 
     barrier = pltpu.get_barrier_semaphore()
-
-    def greet_plane(j, c):
+    for peer in line:
+        pl.semaphore_signal(barrier, inc=1, device_id=(peer, f), device_id_type=MESH)
+    for gx, inner in plane:
         pl.semaphore_signal(
-            barrier, inc=1, device_id=(z, lax.rem(f + j, ns)), device_id_type=MESH
+            barrier, inc=1, device_id=(z, gx * m + inner), device_id_type=MESH
         )
-        return c
-
-    def greet_line(j, c):
-        pl.semaphore_signal(
-            barrier, inc=1, device_id=(lax.rem(z + j, zs), f), device_id_type=MESH
-        )
-        return c
-
-    lax.fori_loop(1, zs, greet_line, 0)
-    lax.fori_loop(1, ns, greet_plane, 0)
 
     own_id = ids_s[0]
     own_pos = pos_s[0]
     own_time = time_s[0]
     id_own[...] = jnp.full(id_own.shape, own_id, jnp.int32)
     id_buf[z] = id_own[...]
+
+    tok_f = tok[...].astype(F32)
+    centre = jnp.mean(tok_f, -1, keepdims=True)
+    spread = jnp.mean((tok_f - centre) ** 2, -1, keepdims=True)
+    tok_hat = ((tok_f - centre) * lax.rsqrt(spread + EPSILON)).astype(BF)
+    at_pos = iota((tok_len, 1), 0) == own_pos
+    lab_lane = iota((tok_len, LANES), 1)
+    lab_row = iota((tok_len, LANES), 0)
+    id_high = lax.div(own_id, 64)
+    id_low = lax.rem(own_id, 64)
+    label = jnp.where(lab_lane == 0, own_time, 0)
+    label = jnp.where((lab_lane == 1) & (lab_row == own_pos), 1, label)
+    label = jnp.where(lab_lane == 2, id_high, label)
+    label = jnp.where(lab_lane == 3, id_low, label)
+    label = label.astype(F32).astype(BF)
+    for c in range(groups):
+        tok_msg[c, :, :group_w] = tok_hat[:, c * group_w : (c + 1) * group_w]
+        tok_msg[c, :, group_w:] = label
+    tok_recv[f] = tok_msg[grp]
+
+    mod32[...] = jnp.zeros(mod32.shape, F32)
+    mod32[:, :, :slice_w] = mods[...].astype(F32)
+    modp[:buckets, :] = mod32[:, 0, :].astype(BF)
+    modp[buckets:, :] = mod32[:, 1, :].astype(BF)
+    mod_recv[r] = modp[...]
+    weight_load.wait()
     w_recv[pl.ds(pl.multiple_of(r * slice_w, 16), slice_w), :] = weight[
         :, pl.ds(pl.multiple_of(r * block, LANES), block)
     ]
-    mod_recv[r] = modp[...]
 
     pl.semaphore_wait(barrier, zs - 1 + ns - 1)
 
@@ -149,25 +197,21 @@
     def drain(ref, phase):
         pltpu.make_async_copy(ref, ref, send_sem.at[phase]).wait()
 
-    def send_id(j, c):
-        remote(id_own, id_buf.at[z], 0, (lax.rem(z + j, zs), f)).start()
-        return c
-
-    lax.fori_loop(1, zs, send_id, 0)
-
-    def send_weight(j, c):
-        peer = lax.rem(r + j, m)
-        device = (z, grp * m + peer)
+    for peer in line:
+        remote(id_own, id_buf.at[z], 0, (peer, f)).start()
+
+    for peer in mates:
+        remote(modp, mod_recv.at[r], 2, (z, grp * m + peer)).start()
+    for peer in mates:
         remote(
             weight.at[:, pl.ds(pl.multiple_of(peer * block, LANES), block)],
             w_recv.at[pl.ds(pl.multiple_of(r * slice_w, 16), slice_w), :],
             1,
-            device,
+            (z, grp * m + peer),
         ).start()
-        remote(modp, mod_recv.at[r], 2, device).start()
-        return c
-
-    lax.fori_loop(1, m, send_weight, 0)
+
+    for gx, inner in plane:
+        remote(tok_msg.at[gx], tok_recv.at[f], 4, (z, gx * m + inner)).start()
 
     for copy in loads:
         copy.wait()
@@ -188,11 +232,7 @@
 
     half = heads // 2
     lax.fori_loop(0, half, image_head, 0)
-
-    tok_f = tok[...].astype(F32)
-    centre = jnp.mean(tok_f, -1, keepdims=True)
-    spread = jnp.mean((tok_f - centre) ** 2, -1, keepdims=True)
-    tok_hat = ((tok_f - centre) * lax.rsqrt(spread + EPSILON)).astype(BF).astype(F32)
+    table_load.wait()
 
     finish(id_buf.at[pl.ds(0, zs - 1)], 0)
     wanted = id_buf[:, 0, :][:, :1]
@@ -202,100 +242,65 @@
         row32[:, c, :] = rows[:, c * LANES : (c + 1) * LANES]
     row_send[...] = row32[...].astype(BF)
     row_recv[z] = row_send[z]
-
-    def send_row(j, c):
-        peer = lax.rem(z + j, zs)
+    for peer in line:
         remote(row_send.at[peer], row_recv.at[z], 3, (peer, f)).start()
-        return c
-
-    lax.fori_loop(1, zs, send_row, 0)
 
     lax.fori_loop(half, heads, image_head, 0)
 
     finish(mod_recv.at[pl.ds(0, m - 1)], 2)
     lane_row = iota((LANES, group_w), 0)
     lane_col = iota((LANES, group_w), 1)
-    mods = jnp.zeros((2 * buckets, group_w), F32)
+    mod_sum = jnp.zeros((2 * buckets, group_w), F32)
     for c in range(m):
         place = ((lane_col == lane_row + c * slice_w) & (lane_row < slice_w)).astype(F32)
-        mods += jnp.dot(mod_recv[c], place.astype(BF), preferred_element_type=F32)
-    mod_all[...] = mods.astype(BF)
+        mod_sum += jnp.dot(mod_recv[c], place.astype(BF), preferred_element_type=F32)
+    mod_all[...] = mod_sum.astype(BF)
 
     table_f = table[...].astype(F32)
     t_centre = jnp.mean(table_f, -1, keepdims=True)
     t_spread = jnp.mean((table_f - t_centre) ** 2, -1, keepdims=True)
     t_rstd = lax.rsqrt(t_spread + EPSILON)
     diag = iota((rows_own, rows_own), 0) == iota((rows_own, rows_own), 1)
-    count_col = jnp.sum(
-        jnp.where(diag, counts[...].astype(F32), 0.0), -1, keepdims=True
-    )
-    own_scale = t_rstd / count_col
+    own_scale = jnp.sum(jnp.where(diag, t_rstd, 0.0), 0, keepdims=True) / counts[...].astype(F32)
+
+    finish(tok_recv.at[pl.ds(0, ns - 1)], 4)
+    all_rows = tok_recv[...].astype(F32).reshape(ns * tok_len, group_w + LANES)
+    toks = all_rows[:, :group_w]
+    labels = all_rows[:, group_w:]
+    times = labels[:, 0:1].astype(jnp.int32)
+    pick_time = (iota((ns * tok_len, buckets), 1) == times).astype(F32).astype(BF)
+    shift = jnp.dot(pick_time, mod_all[:buckets, :], preferred_element_type=F32)
+    scale = 1.0 + jnp.dot(pick_time, mod_all[buckets:, :], preferred_element_type=F32)
+    modulated = (scale * toks + shift).astype(BF)
+    shift_s = shift.reshape(ns, tok_len, group_w)[:, 0, :]
+    scale_s = scale.reshape(ns, tok_len, group_w)[:, 0, :]
+    a_high, a_low = split_two(scale_s)
+    finish(w_recv.at[pl.ds(0, (m - 1) * slice_w)], 1)
+    terms = jnp.dot(modulated, w_recv[...], preferred_element_type=F32)
+    extra = jnp.dot(
+        jnp.concatenate([a_high, a_low], 0), w_recv[...], preferred_element_type=F32
+    )
+    sums = (extra[:ns] + extra[ns:]).reshape(ns, 1, block)
+    placed = labels.reshape(ns, tok_len, LANES)[:, :, 1:2]
+    part[...] = jnp.where(placed > 0.5, sums, terms.reshape(ns, tok_len, block))
+    part_recv[f] = part[f]
+    for gx, inner in plane:
+        peer = gx * m + inner
+        remote(part.at[peer], part_recv.at[f], 5, (z, peer)).start()
 
     finish(row_recv.at[pl.ds(0, zs - 1)], 3)
     concept = jnp.sum(row_recv[...].astype(F32), 0)
     c_mean = jnp.sum(jnp.sum(concept, -1, keepdims=True), 0, keepdims=True) / width
     c_diff = concept - c_mean
     c_var = jnp.sum(jnp.sum(c_diff * c_diff, -1, keepdims=True), 0, keepdims=True) / width
-    c32[...] = c_diff * lax.rsqrt(c_var + EPSILON)
+    c32[...] = (c_diff * lax.rsqrt(c_var + EPSILON)).astype(BF).astype(F32)
     for c in range(width // LANES):
         c_row[:, c * LANES : (c + 1) * LANES] = c32[c : c + 1, :]
-    at_pos = iota((tok_len, 1), 0) == own_pos
-    normed = jnp.where(at_pos, c_row[...], tok_hat).astype(BF)
-    lab_lane = iota((tok_len, LANES), 1)
-    lab_row = iota((tok_len, LANES), 0)
-    id_high = lax.div(own_id, 64)
-    id_low = lax.rem(own_id, 64)
-    label = jnp.where(lab_lane == 0, own_time, 0)
-    label = jnp.where((lab_lane == 1) & (lab_row == own_pos), 1, label)
-    label = jnp.where(lab_lane == 2, id_high, label)
-    label = jnp.where(lab_lane == 3, id_low, label)
-    label = label.astype(F32).astype(BF)
     for c in range(groups):
-        tok_msg[c, :, :group_w] = normed[:, c * group_w : (c + 1) * group_w]
-        tok_msg[c, :, group_w:] = label
-    tok_recv[f] = tok_msg[grp]
-
-    def send_tok(j, c):
-        peer = lax.rem(f + j, ns)
-        remote(tok_msg.at[lax.div(peer, m)], tok_recv.at[f], 4, (z, peer)).start()
-        return c
-
-    lax.fori_loop(1, ns, send_tok, 0)
-    finish(w_recv.at[pl.ds(0, (m - 1) * slice_w)], 1)
-    finish(tok_recv.at[pl.ds(0, ns - 1)], 4)
-
-    all_rows = tok_recv[...].astype(F32).reshape(ns * tok_len, group_w + LANES)
-    toks = all_rows[:, :group_w]
-    labels = all_rows[:, group_w:]
-    times = labels[:, 0:1].astype(jnp.int32)
-    placed = labels[:, 1:2]
-    pick_time = (iota((ns * tok_len, buckets), 1) == times).astype(F32).astype(BF)
-    shift = jnp.dot(pick_time, mod_all[:buckets, :], preferred_element_type=F32)
-    scale = 1.0 + jnp.dot(pick_time, mod_all[buckets:, :], preferred_element_type=F32)
-    modulated = (scale * toks + shift).astype(BF)
-    terms = jnp.dot(modulated, w_recv[...], preferred_element_type=F32)
-    part[...] = terms.reshape(ns, tok_len, block)
-    concepts = jnp.sum((toks * placed).reshape(ns, tok_len, group_w), 1)
-    scales = jnp.sum((scale * placed).reshape(ns, tok_len, group_w), 1)
-    a_high, a_low = split_two(scales)
-    b_high, b_low = split_two(scales * concepts)
-    extra = jnp.dot(
-        jnp.concatenate([a_high, a_low, b_high, b_low], 0),
-        w_recv[...],
-        preferred_element_type=F32,
-    )
-    side[:, 0, :] = extra[:ns] + extra[ns : 2 * ns]
-    side[:, 1, :] = extra[2 * ns : 3 * ns] + extra[3 * ns :]
-    part_recv[f] = part[f]
-    side_recv[f] = side[f]
-
-    def send_part(j, c):
-        peer = lax.rem(f + j, ns)
-        remote(part.at[peer], part_recv.at[f], 5, (z, peer)).start()
-        remote(side.at[peer], side_recv.at[f], 6, (z, peer)).start()
-        return c
-
-    lax.fori_loop(1, ns, send_part, 0)
+        c_msg[c] = c_row[:, c * group_w : (c + 1) * group_w]
+    c_recv[f] = c_msg[grp]
+    for gx, inner in plane:
+        remote(c_msg.at[gx], c_recv.at[f], 9, (z, gx * m + inner)).start()
 
     labels_s = labels.reshape(ns, tok_len, LANES)[:, 0, :]
     pick_s = (
@@ -305,24 +310,41 @@
     own_row = iota((group_w, LANES), 0)
     own_col = iota((group_w, LANES), 1)
     own_place = ((own_row == own_col + r * slice_w) & (own_col < slice_w)).astype(F32).astype(BF)
+
+    finish(c_recv.at[pl.ds(0, ns - 1)], 9)
+    concepts = c_recv[:, 0, :]
+    scaled = scale_s * concepts
+    b_high, b_low = split_two(scaled)
+    extra = jnp.dot(
+        jnp.concatenate([(scaled + shift_s).astype(BF), b_high, b_low], 0),
+        w_recv[...],
+        preferred_element_type=F32,
+    )
+    late[:, 0, :] = extra[:ns]
+    late[:, 1, :] = extra[ns : 2 * ns] + extra[2 * ns :]
+    late_recv[f] = late[f]
+    for gx, inner in plane:
+        peer = gx * m + inner
+        remote(late.at[peer], late_recv.at[f], 6, (z, peer)).start()
     concept_own = jnp.dot(concepts.astype(BF), own_place, preferred_element_type=F32)
 
     finish(part_recv.at[pl.ds(0, ns - 1)], 5)
-    finish(side_recv.at[pl.ds(0, ns - 1)], 6)
+    finish(late_recv.at[pl.ds(0, ns - 1)], 6)
     per = block // LANES
+    pos_f = at_pos.astype(F32)
     for c in range(m):
         total = part_recv[c]
-        extras = side_recv[c]
+        extras = late_recv[c]
         for a in range(1, groups):
             total += part_recv[a * m + c]
-            extras += side_recv[a * m + c]
-        kv[:, c * block : (c + 1) * block] = total
+            extras += late_recv[a * m + c]
+        first = jnp.sum(total * pos_f, 0, keepdims=True)
+        kv[:, c * block : (c + 1) * block] = jnp.where(at_pos, extras[0:1, :], total)
         for b in range(per):
-            s1_32[c * per + b : c * per + b + 1, :] = extras[0:1, b * LANES : (b + 1) * LANES]
+            s1_32[c * per + b : c * per + b + 1, :] = first[:, b * LANES : (b + 1) * LANES]
             s2_32[c * per + b : c * per + b + 1, :] = extras[1:2, b * LANES : (b + 1) * LANES]
 
     kv_all = kv[...] + bias[...]
-    pos_f = at_pos.astype(F32)
     gains = gain[...]
     raw_row = jnp.sum(kv_all[:, :head_w] * pos_f, 0, keepdims=True)
     key_parts = []
@@ -391,11 +413,8 @@
     dkv_own[...] = dkv32[...].astype(BF)
     dkv_recv[f] = dkv_own[...]
 
-    def send_dkv(j, c):
-        remote(dkv_own, dkv_recv.at[f], 7, (z, lax.rem(f + j, ns))).start()
-        return c
-
-    lax.fori_loop(1, ns, send_dkv, 0)
+    for gx, inner in plane:
+        remote(dkv_own, dkv_recv.at[f], 7, (z, gx * m + inner)).start()
     finish(dkv_recv.at[pl.ds(0, ns - 1)], 7)
     dkv_wide[...] = dkv_recv[...].astype(F32)
     grads = jnp.zeros((ns, slice_w), F32)
@@ -414,11 +433,8 @@
     g_own[:, slice_w:] = labels_s[:, : LANES - slice_w].astype(BF)
     g_recv[z] = g_own[...]
 
-    def send_grad(j, c):
-        remote(g_own, g_recv.at[z], 8, (lax.rem(z + j, zs), f)).start()
-        return c
-
-    lax.fori_loop(1, zs, send_grad, 0)
+    for peer in line:
+        remote(g_own, g_recv.at[z], 8, (peer, f)).start()
     finish(g_recv.at[pl.ds(0, zs - 1)], 8)
     every = g_recv[...].astype(F32).reshape(zs * ns, LANES)
     who = (every[:, slice_w + 2 : slice_w + 3] * 64.0 + every[:, slice_w + 3 : slice_w + 4]).astype(
@@ -426,9 +442,9 @@
     )
     belongs = (iota((zs * ns, rows_own), 1) + z * rows_own == who).astype(F32).astype(BF)
     summed = lax.dot_general(
-        belongs, every.astype(BF), TN_DIMS, preferred_element_type=F32
-    )
-    out[...] = (summed * own_scale)[:, :slice_w]
+        every.astype(BF), belongs, TN_DIMS, preferred_element_type=F32
+    )
+    out[...] = summed[:slice_w, :] * own_scale
 
     drain(id_buf.at[pl.ds(0, zs - 1)], 0)
     drain(w_recv.at[pl.ds(0, (m - 1) * slice_w)], 1)
@@ -436,9 +452,10 @@
     drain(row_recv.at[pl.ds(0, zs - 1)], 3)
     drain(tok_recv.at[pl.ds(0, ns - 1)], 4)
     drain(part_recv.at[pl.ds(0, ns - 1)], 5)
-    drain(side_recv.at[pl.ds(0, ns - 1)], 6)
+    drain(late_recv.at[pl.ds(0, ns - 1)], 6)
     drain(dkv_recv.at[pl.ds(0, ns - 1)], 7)
     drain(g_recv.at[pl.ds(0, zs - 1)], 8)
+    drain(c_recv.at[pl.ds(0, ns - 1)], 9)
 
 
 def shards(
@@ -459,7 +476,8 @@
 ):
     ns = lax.axis_size("fsdp")
     zs = lax.axis_size("dp")
-    m = 8 if ns % 16 == 0 else 4
+    nx, ny = (4, 4) if ns == 32 else (2, 2)
+    m = ny * 2
     tok_len, width = txt_tokens.shape[1:]
     slice_w, kv_w = kv_weight.shape
     head_w = kv_w // 2
@@ -472,24 +490,25 @@
     n_c = width // LANES
     slot = (2 * heads + 4 + 15) // 16 * 16
 
-    modp = jnp.pad(
-        mod_table.transpose(1, 0, 2).reshape(2 * buckets, slice_w), ((0, 0), (0, LANES - slice_w))
-    )
     vm = pl.BlockSpec(memory_space=pltpu.VMEM)
     sm = pl.BlockSpec(memory_space=pltpu.SMEM)
     hb = pl.BlockSpec(memory_space=pl.ANY)
     image = pltpu.VMEM((n_img, head_w), BF)
     stat = pltpu.VMEM((heads, 1, n_img), F32)
-    return pl.pallas_call(
-        functools.partial(step_kernel, (zs, ns, m)),
-        out_shape=jax.ShapeDtypeStruct((rows_own, slice_w), F32),
-        in_specs=[sm] * 3 + [vm] * 7 + [hb] * 4,
+    grad_t = pl.pallas_call(
+        functools.partial(step_kernel, (zs, nx, ny)),
+        out_shape=jax.ShapeDtypeStruct((slice_w, rows_own), F32),
+        in_specs=[sm] * 3 + [vm] * 5 + [hb] * 6,
         out_specs=vm,
         scratch_shapes=[
+            pltpu.VMEM((rows_own, width), BF),
+            pltpu.VMEM((slice_w, kv_w), BF),
             image,
             image,
             image,
             image,
+            pltpu.VMEM((buckets, 2, LANES), F32),
+            pltpu.VMEM((2 * buckets, LANES), BF),
             pltpu.VMEM((zs, 1, LANES), jnp.int32),
             pltpu.VMEM((1, LANES), jnp.int32),
             pltpu.VMEM((zs, n_c, LANES), F32),
@@ -499,6 +518,8 @@
             pltpu.VMEM((1, width), F32),
             pltpu.VMEM((ns // m, tok_len, group_w + LANES), BF),
             pltpu.VMEM((ns, tok_len, group_w + LANES), BF),
+            pltpu.VMEM((nx, 1, group_w), F32),
+            pltpu.VMEM((ns, 1, group_w), F32),
             pltpu.VMEM((group_w, block), BF),
             pltpu.VMEM((m, 2 * buckets, LANES), BF),
             pltpu.VMEM((2 * buckets, group_w), BF),
@@ -519,9 +540,9 @@
             pltpu.VMEM((ns, slot, LANES), F32),
             pltpu.VMEM((ns, LANES), BF),
             pltpu.VMEM((zs, ns, LANES), BF),
-            pltpu.SemaphoreType.DMA((4,)),
-            pltpu.SemaphoreType.DMA((9,)),
-            pltpu.SemaphoreType.DMA((9,)),
+            pltpu.SemaphoreType.DMA((6,)),
+            pltpu.SemaphoreType.DMA((10,)),
+            pltpu.SemaphoreType.DMA((10,)),
         ],
         compiler_params=pltpu.CompilerParams(collective_id=0, has_side_effects=True),
     )(
@@ -529,17 +550,18 @@
         positions,
         timesteps,
         txt_tokens[0],
-        concept_table,
         counts[None, :],
-        modp,
-        kv_weight,
+        mod_table,
         kv_bias[None, :],
         key_gain[None, :],
+        concept_table,
+        kv_weight,
         img_query[0],
         img_key[0],
         img_value[0],
         out_grad[0],
     )
+    return grad_t.T
 
 
 def solution(mesh):

time: 75.9 us -> 69 us (0.909)
  the two profiles are of different devices: /device:TPU:4 before, /device:TPU:1 now
where the time goes in v2:
time: 69 us; the launch traced here: 68.8 us
  Pallas kernels  65.3 us (95%)
  between operations  1.95 us (3%)
  local copies, waits for them, and re-layouts  1.54 us (2%)
    pallas_call x1, Pallas kernels, shards(): pl.pallas_call(functools.partial(step_kernel, (zs, nx, ny)), out_shape=ja...  65.3 us
    unnamed x1, local copies, waits for them, and re-layouts  1.54 us

profile of v2, /device:TPU:1, one launch (start us, length us, event | category | flops | bytes accessed | tf_op | source)
XLA Modules:
  0.0 68.8 jit_solution(11705753023967091235)
XLA Ops:
  1.9 65.3 %shard_map.136 = f32[96,256]{1,0:T(8,128)} custom-call(s32[1]{0:T(128)S(6)} %copy.16.ids_s, s32[1]{0:T(128)S(6)} %copy.17.pos_s, s32[1]{0:T(128)S(6)} %copy.18.time_s, bf16[8,3072]{1,0:T(8,128)(2,1)} %bitcast.14, s32[1,256]{1,0:T(1,128)} %bitcast.16, bf16[64,2,96]{2,1,0:T(2,128)(2,1)} %mods.1, f32[1,3072]{1,0:T(1,128)} %bitcast.15, f32[1,128]{1,0:T(1,128)} %bitcast.17, ...), custom_call_target="tpu_custom_call" | custom-call | tf_op jit(solution)/shard_map/pallas_call | solution.py:498
  67.2 1.5 %copy.19 = f32[256,96]{0,1:T(8,128)} copy(f32[256,96]{0,1:T(8,128)} %bitcast.13) | data formatting | bytes 196608

commit v3 on v2

--- a/solution.py
+++ b/solution.py
@@ -39,11 +39,11 @@
     ids_s,
     pos_s,
     time_s,
-    tok,
-    counts,
-    mods,
-    bias,
-    gain,
+    tok_any,
+    counts_any,
+    mods_any,
+    bias_any,
+    gain_any,
     table_any,
     weight_any,
     q_any,
@@ -51,6 +51,11 @@
     v_any,
     g_any,
     out,
+    tok,
+    counts,
+    mods,
+    bias,
+    gain,
     table,
     weight,
     q,
@@ -59,6 +64,12 @@
     g,
     mod32,
     modp,
+    lab_own,
+    lab_recv,
+    idz_own,
+    idz_recv,
+    belongs_a,
+    belongs_b,
     id_buf,
     id_own,
     row32,
@@ -66,13 +77,15 @@
     row_recv,
     c32,
     c_row,
+    cut_a,
+    cut_b,
     tok_msg,
     tok_recv,
     c_msg,
     c_recv,
+    w_t,
     w_recv,
     mod_recv,
-    mod_all,
     part,
     part_recv,
     late,
@@ -88,6 +101,7 @@
     dkv_own,
     dkv_recv,
     dkv_wide,
+    g32,
     g_own,
     g_recv,
     load_sem,
@@ -100,8 +114,9 @@
     z = lax.axis_index("dp")
     f = lax.axis_index("fsdp")
     groups = nx
-    r = lax.rem(f, m)
-    grp = lax.div(f, m)
+    my_x = lax.div(f, m)
+    my_y = lax.div(lax.rem(f, m), 2)
+    my_c = lax.rem(f, 2)
     tok_len, width = tok.shape
     slice_w = weight.shape[0]
     kv_w = weight.shape[1]
@@ -114,35 +129,68 @@
     buckets = mods.shape[0]
     inv_root = 1.0 / (LANES**0.5)
 
-    my_y = lax.div(r, 2)
-    my_c = lax.rem(r, 2)
-    x_at = [lax.rem(grp + d, nx) for d in range(nx)]
-    y_at = [lax.rem(my_y + d, ny) * 2 for d in range(ny)]
+    x_at = [lax.rem(my_x + d, nx) for d in range(nx)]
+    y_at = [lax.rem(my_y + d, ny) for d in range(ny)]
     c_at = [my_c, 1 - my_c]
-    plane = [(x_at[a], y_at[b] + c_at[c]) for a, b, c in far_first((nx, ny))]
-    mates = [y_at[b] + c_at[c] for a, b, c in far_first((nx, ny)) if a == 0]
+    chips = nx * ny
+    plane = [
+        ((x_at[a] * ny + y_at[b]) * 2 + c_at[c], c_at[c] * chips + x_at[a] * ny + y_at[b])
+        for a, b, c in far_first((nx, ny))
+    ]
+    same_core = [
+        ((x_at[a] * ny + y_at[b]) * 2 + my_c, x_at[a] * ny + y_at[b])
+        for a, b, c in far_first((nx, ny))
+        if c == 0
+    ]
+    chip_of = [x_at[a] * ny + y_at[b] for a, b, c in far_first((nx, ny))]
+    me_chip = my_x * ny + my_y
+    me = my_c * chips + me_chip
+    from_me = my_x * m + lax.rem(my_x + my_y, ny) * 2 + my_c
+    ring = my_x * (1 - my_c) + my_y * my_c
+    own_slot = my_c * nx + ring
+    own_block = lax.rem(my_x + my_y, ny) * 2 + my_c
+    mates = []
+    for b, c in sorted(
+        ((b, c) for b in range(ny) for c in range(2)), key=lambda bc: -min(bc[0], ny - bc[0])
+    ):
+        if b or c:
+            mate_x = lax.rem(my_x + b * (1 - my_c), nx)
+            mate_y = lax.rem(my_y + b * my_c, ny)
+            mates.append(
+                (
+                    (mate_x * ny + mate_y) * 2 + c_at[c],
+                    lax.rem(mate_x + mate_y, ny) * 2 + c_at[c],
+                )
+            )
     line = [
         lax.rem(z + d, zs) for d in sorted(range(1, zs), key=lambda d: (-min(d, zs - d), d))
     ]
 
-    table_load = pltpu.make_async_copy(table_any, table, load_sem.at[0])
-    weight_load = pltpu.make_async_copy(weight_any, weight, load_sem.at[1])
-    loads = [
-        pltpu.make_async_copy(src, dst, load_sem.at[2 + i])
-        for i, (src, dst) in enumerate(((q_any, q), (k_any, k), (v_any, v), (g_any, g)))
-    ]
-    weight_load.start()
-    table_load.start()
-    for copy in loads:
-        copy.start()
-
     barrier = pltpu.get_barrier_semaphore()
     for peer in line:
         pl.semaphore_signal(barrier, inc=1, device_id=(peer, f), device_id_type=MESH)
-    for gx, inner in plane:
-        pl.semaphore_signal(
-            barrier, inc=1, device_id=(z, gx * m + inner), device_id_type=MESH
-        )
+
+    pairs = (
+        (tok_any, tok),
+        (mods_any, mods),
+        (weight_any, weight),
+        (q_any, q),
+        (k_any, k),
+        (v_any, v),
+        (g_any, g),
+        (table_any, table),
+        (counts_any, counts),
+        (bias_any, bias),
+        (gain_any, gain),
+    )
+    loads = [
+        pltpu.make_async_copy(src, dst, load_sem.at[i]) for i, (src, dst) in enumerate(pairs)
+    ]
+    for copy in loads:
+        copy.start()
+
+    for peer, _ in plane:
+        pl.semaphore_signal(barrier, inc=1, device_id=(z, peer), device_id_type=MESH)
 
     own_id = ids_s[0]
     own_pos = pos_s[0]
@@ -150,33 +198,40 @@
     id_own[...] = jnp.full(id_own.shape, own_id, jnp.int32)
     id_buf[z] = id_own[...]
 
+    lane = iota((1, LANES), 1)
+    label = jnp.where(lane == 0, own_time, jnp.where(lane == 1, own_pos, own_id))
+    lab_own[...] = label.astype(F32)
+    lab_recv[me] = lab_own[...]
+    at_pos = iota((tok_len, 1), 0) == own_pos
+
+    loads[0].wait()
     tok_f = tok[...].astype(F32)
     centre = jnp.mean(tok_f, -1, keepdims=True)
     spread = jnp.mean((tok_f - centre) ** 2, -1, keepdims=True)
     tok_hat = ((tok_f - centre) * lax.rsqrt(spread + EPSILON)).astype(BF)
-    at_pos = iota((tok_len, 1), 0) == own_pos
-    lab_lane = iota((tok_len, LANES), 1)
-    lab_row = iota((tok_len, LANES), 0)
-    id_high = lax.div(own_id, 64)
-    id_low = lax.rem(own_id, 64)
-    label = jnp.where(lab_lane == 0, own_time, 0)
-    label = jnp.where((lab_lane == 1) & (lab_row == own_pos), 1, label)
-    label = jnp.where(lab_lane == 2, id_high, label)
-    label = jnp.where(lab_lane == 3, id_low, label)
-    label = label.astype(F32).astype(BF)
-    for c in range(groups):
-        tok_msg[c, :, :group_w] = tok_hat[:, c * group_w : (c + 1) * group_w]
-        tok_msg[c, :, group_w:] = label
-    tok_recv[f] = tok_msg[grp]
+    half_w = nx * slice_w
+    tok_32 = tok_hat.astype(F32)
+    for a in range(nx):
+        for b in range(ny):
+            at = (a * ny + b) * 2 * slice_w
+            cut_a[b, :, a * slice_w : (a + 1) * slice_w] = tok_32[:, at : at + slice_w]
+            at += slice_w
+            cut_b[a, :, b * slice_w : (b + 1) * slice_w] = tok_32[:, at : at + slice_w]
+    for a in range(nx):
+        for b in range(ny):
+            tok_msg[a * ny + b, :, :half_w] = cut_a[b].astype(BF)
+            tok_msg[a * ny + b, :, half_w:] = cut_b[a].astype(BF)
+    tok_recv[my_c, me_chip] = tok_msg[me_chip]
 
     mod32[...] = jnp.zeros(mod32.shape, F32)
+    loads[1].wait()
     mod32[:, :, :slice_w] = mods[...].astype(F32)
     modp[:buckets, :] = mod32[:, 0, :].astype(BF)
     modp[buckets:, :] = mod32[:, 1, :].astype(BF)
-    mod_recv[r] = modp[...]
-    weight_load.wait()
-    w_recv[pl.ds(pl.multiple_of(r * slice_w, 16), slice_w), :] = weight[
-        :, pl.ds(pl.multiple_of(r * block, LANES), block)
+    mod_recv[own_slot] = modp[...]
+    loads[2].wait()
+    w_recv[pl.ds(pl.multiple_of(own_slot * slice_w, 16), slice_w), :] = weight[
+        :, pl.ds(pl.multiple_of(own_block * block, LANES), block)
     ]
 
     pl.semaphore_wait(barrier, zs - 1 + ns - 1)
@@ -200,20 +255,24 @@
     for peer in line:
         remote(id_own, id_buf.at[z], 0, (peer, f)).start()
 
-    for peer in mates:
-        remote(modp, mod_recv.at[r], 2, (z, grp * m + peer)).start()
-    for peer in mates:
+    for peer, _ in plane:
+        remote(lab_own, lab_recv.at[me], 10, (z, peer)).start()
+
+    for peer, chip in same_core:
+        remote(tok_msg.at[chip], tok_recv.at[my_c, me_chip], 4, (z, peer)).start()
+
+    for peer, _ in mates:
+        remote(modp, mod_recv.at[own_slot], 2, (z, peer)).start()
+
+    for peer, theirs in mates:
         remote(
-            weight.at[:, pl.ds(pl.multiple_of(peer * block, LANES), block)],
-            w_recv.at[pl.ds(pl.multiple_of(r * slice_w, 16), slice_w), :],
+            weight.at[:, pl.ds(pl.multiple_of(theirs * block, LANES), block)],
+            w_recv.at[pl.ds(pl.multiple_of(own_slot * slice_w, 16), slice_w), :],
             1,
-            (z, grp * m + peer),
+            (z, peer),
         ).start()
 
-    for gx, inner in plane:
-        remote(tok_msg.at[gx], tok_recv.at[f], 4, (z, gx * m + inner)).start()
-
-    for copy in loads:
+    for copy in loads[3:]:
         copy.wait()
 
     def image_head(h, c):
@@ -232,7 +291,6 @@
 
     half = heads // 2
     lax.fori_loop(0, half, image_head, 0)
-    table_load.wait()
 
     finish(id_buf.at[pl.ds(0, zs - 1)], 0)
     wanted = id_buf[:, 0, :][:, :1]
@@ -245,7 +303,28 @@
     for peer in line:
         remote(row_send.at[peer], row_recv.at[z], 3, (peer, f)).start()
 
+    finish(lab_recv.at[pl.ds(0, ns - 1)], 10)
+    labels = lab_recv[:, 0, :]
+    pick_s = (iota((ns, buckets), 1) == labels[:, 0:1].astype(jnp.int32)).astype(F32).astype(BF)
+    scale_own = 1.0 + jnp.dot(pick_s, modp[buckets:, :], preferred_element_type=F32)
+
+    sample_diag = iota((ns, LANES), 0) == iota((ns, LANES), 1)
+    idz_own[...] = jnp.sum(jnp.where(sample_diag, labels[:, 2:3], 0.0), 0, keepdims=True)
+    idz_recv[z] = idz_own[...]
+    for peer in line:
+        remote(idz_own, idz_recv.at[z], 11, (peer, f)).start()
+
+    finish(tok_recv.at[0, pl.ds(0, chips - 1)], 4)
+    remote(tok_recv.at[my_c], tok_recv.at[my_c], 12, (z, f + 1 - 2 * my_c)).start()
+
     lax.fori_loop(half, heads, image_head, 0)
+
+    table_f = table[...].astype(F32)
+    t_centre = jnp.mean(table_f, -1, keepdims=True)
+    t_spread = jnp.mean((table_f - t_centre) ** 2, -1, keepdims=True)
+    t_rstd = lax.rsqrt(t_spread + EPSILON)
+    diag = iota((rows_own, rows_own), 0) == iota((rows_own, rows_own), 1)
+    own_scale = jnp.sum(jnp.where(diag, t_rstd, 0.0), 0, keepdims=True) / counts[...].astype(F32)
 
     finish(mod_recv.at[pl.ds(0, m - 1)], 2)
     lane_row = iota((LANES, group_w), 0)
@@ -254,39 +333,28 @@
     for c in range(m):
         place = ((lane_col == lane_row + c * slice_w) & (lane_row < slice_w)).astype(F32)
         mod_sum += jnp.dot(mod_recv[c], place.astype(BF), preferred_element_type=F32)
-    mod_all[...] = mod_sum.astype(BF)
-
-    table_f = table[...].astype(F32)
-    t_centre = jnp.mean(table_f, -1, keepdims=True)
-    t_spread = jnp.mean((table_f - t_centre) ** 2, -1, keepdims=True)
-    t_rstd = lax.rsqrt(t_spread + EPSILON)
-    diag = iota((rows_own, rows_own), 0) == iota((rows_own, rows_own), 1)
-    own_scale = jnp.sum(jnp.where(diag, t_rstd, 0.0), 0, keepdims=True) / counts[...].astype(F32)
-
-    finish(tok_recv.at[pl.ds(0, ns - 1)], 4)
-    all_rows = tok_recv[...].astype(F32).reshape(ns * tok_len, group_w + LANES)
-    toks = all_rows[:, :group_w]
-    labels = all_rows[:, group_w:]
-    times = labels[:, 0:1].astype(jnp.int32)
-    pick_time = (iota((ns * tok_len, buckets), 1) == times).astype(F32).astype(BF)
-    shift = jnp.dot(pick_time, mod_all[:buckets, :], preferred_element_type=F32)
-    scale = 1.0 + jnp.dot(pick_time, mod_all[buckets:, :], preferred_element_type=F32)
-    modulated = (scale * toks + shift).astype(BF)
-    shift_s = shift.reshape(ns, tok_len, group_w)[:, 0, :]
-    scale_s = scale.reshape(ns, tok_len, group_w)[:, 0, :]
+    shift_s = jnp.dot(pick_s, mod_sum[:buckets].astype(BF), preferred_element_type=F32)
+    scale_s = 1.0 + jnp.dot(pick_s, mod_sum[buckets:].astype(BF), preferred_element_type=F32)
+
+    finish(tok_recv.at[0], 12)
+    toks = tok_recv[...].astype(F32).reshape(ns, tok_len, group_w)
+    modulated = scale_s.reshape(ns, 1, group_w) * toks + shift_s.reshape(ns, 1, group_w)
     a_high, a_low = split_two(scale_s)
+    placed = iota((ns, tok_len, 1), 1) == lab_recv[:, :, 1:2].astype(jnp.int32)
     finish(w_recv.at[pl.ds(0, (m - 1) * slice_w)], 1)
-    terms = jnp.dot(modulated, w_recv[...], preferred_element_type=F32)
+    terms = jnp.dot(
+        modulated.reshape(ns * tok_len, group_w).astype(BF),
+        w_recv[...],
+        preferred_element_type=F32,
+    )
     extra = jnp.dot(
         jnp.concatenate([a_high, a_low], 0), w_recv[...], preferred_element_type=F32
     )
     sums = (extra[:ns] + extra[ns:]).reshape(ns, 1, block)
-    placed = labels.reshape(ns, tok_len, LANES)[:, :, 1:2]
-    part[...] = jnp.where(placed > 0.5, sums, terms.reshape(ns, tok_len, block))
-    part_recv[f] = part[f]
-    for gx, inner in plane:
-        peer = gx * m + inner
-        remote(part.at[peer], part_recv.at[f], 5, (z, peer)).start()
+    part[...] = jnp.where(placed, sums, terms.reshape(ns, tok_len, block))
+    part_recv[from_me] = part[me]
+    for peer, slot in plane:
+        remote(part.at[slot], part_recv.at[from_me], 5, (z, peer)).start()
 
     finish(row_recv.at[pl.ds(0, zs - 1)], 3)
     concept = jnp.sum(row_recv[...].astype(F32), 0)
@@ -296,20 +364,23 @@
     c32[...] = (c_diff * lax.rsqrt(c_var + EPSILON)).astype(BF).astype(F32)
     for c in range(width // LANES):
         c_row[:, c * LANES : (c + 1) * LANES] = c32[c : c + 1, :]
-    for c in range(groups):
-        c_msg[c] = c_row[:, c * group_w : (c + 1) * group_w]
-    c_recv[f] = c_msg[grp]
-    for gx, inner in plane:
-        remote(c_msg.at[gx], c_recv.at[f], 9, (z, gx * m + inner)).start()
-
-    labels_s = labels.reshape(ns, tok_len, LANES)[:, 0, :]
-    pick_s = (
-        (iota((ns, buckets), 1) == labels_s[:, 0:1].astype(jnp.int32)).astype(F32).astype(BF)
-    )
-    scale_own = 1.0 + jnp.dot(pick_s, modp[buckets:, :], preferred_element_type=F32)
+    for a in range(nx):
+        for b in range(ny):
+            at = (a * ny + b) * 2 * slice_w
+            cut_a[b, 0:1, a * slice_w : (a + 1) * slice_w] = c_row[:, at : at + slice_w]
+            at += slice_w
+            cut_b[a, 0:1, b * slice_w : (b + 1) * slice_w] = c_row[:, at : at + slice_w]
+    for a in range(nx):
+        for b in range(ny):
+            c_msg[a * ny + b, :, :half_w] = cut_a[b, 0:1, :]
+            c_msg[a * ny + b, :, half_w:] = cut_b[a, 0:1, :]
+    c_recv[me] = c_msg[me_chip]
+    for (peer, _), chip in zip(plane, chip_of):
+        remote(c_msg.at[chip], c_recv.at[me], 9, (z, peer)).start()
+
     own_row = iota((group_w, LANES), 0)
     own_col = iota((group_w, LANES), 1)
-    own_place = ((own_row == own_col + r * slice_w) & (own_col < slice_w)).astype(F32).astype(BF)
+    own_place = ((own_row == own_col + own_slot * slice_w) & (own_col < slice_w)).astype(F32).astype(BF)
 
     finish(c_recv.at[pl.ds(0, ns - 1)], 9)
     concepts = c_recv[:, 0, :]
@@ -322,11 +393,31 @@
     )
     late[:, 0, :] = extra[:ns]
     late[:, 1, :] = extra[ns : 2 * ns] + extra[2 * ns :]
-    late_recv[f] = late[f]
-    for gx, inner in plane:
-        peer = gx * m + inner
-        remote(late.at[peer], late_recv.at[f], 6, (z, peer)).start()
+    late_recv[from_me] = late[me]
+    for peer, slot in plane:
+        remote(late.at[slot], late_recv.at[from_me], 6, (z, peer)).start()
     concept_own = jnp.dot(concepts.astype(BF), own_place, preferred_element_type=F32)
+
+    finish(idz_recv.at[pl.ds(0, zs - 1)], 11)
+    id_cols = jnp.sum(
+        jnp.where(sample_diag.reshape(1, ns, LANES), idz_recv[...], 0.0), -1, keepdims=True
+    ).astype(jnp.int32)
+    belongs = (iota((zs, ns, rows_own), 2) + z * rows_own == id_cols).astype(F32)
+    half_n, quarter = ns // 2, ns // 4
+    for c in range(2):
+        belongs_a[:, c * rows_own : (c + 1) * rows_own] = (
+            belongs[:, c * half_n : (c + 1) * half_n, :].reshape(zs * half_n, rows_own).astype(BF)
+        )
+    for c in range(4):
+        belongs_b[:, c * rows_own : (c + 1) * rows_own] = (
+            belongs[:, c * quarter : (c + 1) * quarter, :]
+            .reshape(zs * quarter, rows_own)
+            .astype(BF)
+        )
+
+    for c in range(2 * heads):
+        lanes = slice(c * LANES, (c + 1) * LANES)
+        w_t[lanes, :] = weight[:, lanes].astype(F32).T.astype(BF)
 
     finish(part_recv.at[pl.ds(0, ns - 1)], 5)
     finish(late_recv.at[pl.ds(0, ns - 1)], 6)
@@ -411,51 +502,65 @@
         dkv32[at : at + 1, :] = jnp.broadcast_to(high.astype(F32), (1, LANES))
         dkv32[at + 1 : at + 2, :] = jnp.broadcast_to(low.astype(F32), (1, LANES))
     dkv_own[...] = dkv32[...].astype(BF)
-    dkv_recv[f] = dkv_own[...]
-
-    for gx, inner in plane:
-        remote(dkv_own, dkv_recv.at[f], 7, (z, gx * m + inner)).start()
+    dkv_recv[me] = dkv_own[...]
+
+    for peer, _ in plane:
+        remote(dkv_own, dkv_recv.at[me], 7, (z, peer)).start()
     finish(dkv_recv.at[pl.ds(0, ns - 1)], 7)
     dkv_wide[...] = dkv_recv[...].astype(F32)
     grads = jnp.zeros((ns, slice_w), F32)
-    for c in range(2 * heads):
-        grads += lax.dot_general(
-            dkv_wide[:, c, :].astype(BF),
-            weight[:, c * LANES : (c + 1) * LANES],
-            NT_DIMS,
-            preferred_element_type=F32,
+    for c in range(0, 2 * heads, 2):
+        both = jnp.concatenate([dkv_wide[:, c, :], dkv_wide[:, c + 1, :]], 1).astype(BF)
+        grads += jnp.dot(
+            both, w_t[c * LANES : (c + 2) * LANES, :], preferred_element_type=F32
         )
     at = 2 * heads
     mean_1 = (dkv_wide[:, at, :] + dkv_wide[:, at + 1, :])[:, :slice_w]
     mean_2 = (dkv_wide[:, at + 2, :] + dkv_wide[:, at + 3, :])[:, :slice_w]
     row_grad = grads * scale_own[:, :slice_w] - mean_1 - concept_own[:, :slice_w] * mean_2
-    g_own[:, :slice_w] = row_grad.astype(BF)
-    g_own[:, slice_w:] = labels_s[:, : LANES - slice_w].astype(BF)
+    for c in range(2):
+        g32[:half_n, c * 64 : c * 64 + 64] = row_grad[c * half_n : (c + 1) * half_n, :64]
+    for c in range(4):
+        g32[half_n:, c * 32 : c * 32 + 32] = row_grad[c * quarter : (c + 1) * quarter, 64:]
+    g_own[...] = g32[...].astype(BF)
     g_recv[z] = g_own[...]
 
     for peer in line:
         remote(g_own, g_recv.at[z], 8, (peer, f)).start()
     finish(g_recv.at[pl.ds(0, zs - 1)], 8)
-    every = g_recv[...].astype(F32).reshape(zs * ns, LANES)
-    who = (every[:, slice_w + 2 : slice_w + 3] * 64.0 + every[:, slice_w + 3 : slice_w + 4]).astype(
-        jnp.int32
-    )
-    belongs = (iota((zs * ns, rows_own), 1) + z * rows_own == who).astype(F32).astype(BF)
-    summed = lax.dot_general(
-        every.astype(BF), belongs, TN_DIMS, preferred_element_type=F32
-    )
-    out[...] = summed[:slice_w, :] * own_scale
+    wide = g_recv[...].astype(F32)
+    sum_a = lax.dot_general(
+        wide[:, :half_n, :].reshape(zs * half_n, LANES).astype(BF),
+        belongs_a[...],
+        TN_DIMS,
+        preferred_element_type=F32,
+    )
+    sum_b = lax.dot_general(
+        wide[:, half_n:, :].reshape(zs * quarter, LANES).astype(BF),
+        belongs_b[...],
+        TN_DIMS,
+        preferred_element_type=F32,
+    )
+    top_rows = sum_a[:64, :rows_own] + sum_a[64:, rows_own:]
+    low_rows = sum_b[:32, :rows_own]
+    for c in range(1, 4):
+        low_rows += sum_b[c * 32 : c * 32 + 32, c * rows_own : (c + 1) * rows_own]
+    out[:64, :] = top_rows * own_scale
+    out[64:, :] = low_rows * own_scale
 
     drain(id_buf.at[pl.ds(0, zs - 1)], 0)
     drain(w_recv.at[pl.ds(0, (m - 1) * slice_w)], 1)
     drain(mod_recv.at[pl.ds(0, m - 1)], 2)
     drain(row_recv.at[pl.ds(0, zs - 1)], 3)
-    drain(tok_recv.at[pl.ds(0, ns - 1)], 4)
+    drain(tok_recv.at[0, pl.ds(0, chips - 1)], 4)
+    drain(tok_recv.at[0], 12)
     drain(part_recv.at[pl.ds(0, ns - 1)], 5)
     drain(late_recv.at[pl.ds(0, ns - 1)], 6)
     drain(dkv_recv.at[pl.ds(0, ns - 1)], 7)
     drain(g_recv.at[pl.ds(0, zs - 1)], 8)
     drain(c_recv.at[pl.ds(0, ns - 1)], 9)
+    drain(lab_recv.at[pl.ds(0, ns - 1)], 10)
+    drain(idz_recv.at[pl.ds(0, zs - 1)], 11)
 
 
 def shards(
@@ -498,9 +603,14 @@
     grad_t = pl.pallas_call(
         functools.partial(step_kernel, (zs, nx, ny)),
         out_shape=jax.ShapeDtypeStruct((slice_w, rows_own), F32),
-        in_specs=[sm] * 3 + [vm] * 5 + [hb] * 6,
+        in_specs=[sm] * 3 + [hb] * 11,
         out_specs=vm,
         scratch_shapes=[
+            pltpu.VMEM((tok_len, width), BF),
+            pltpu.VMEM((1, rows_own), jnp.int32),
+            pltpu.VMEM((buckets, 2, slice_w), BF),
+            pltpu.VMEM((1, kv_w), F32),
+            pltpu.VMEM((1, LANES), F32),
             pltpu.VMEM((rows_own, width), BF),
             pltpu.VMEM((slice_w, kv_w), BF),
             image,
@@ -509,6 +619,12 @@
             image,
             pltpu.VMEM((buckets, 2, LANES), F32),
             pltpu.VMEM((2 * buckets, LANES), BF),
+            pltpu.VMEM((1, LANES), F32),
+            pltpu.VMEM((ns, 1, LANES), F32),
+            pltpu.VMEM((1, LANES), F32),
+            pltpu.VMEM((zs, 1, LANES), F32),
+            pltpu.VMEM((zs * ns // 2, 2 * rows_own), BF),
+            pltpu.VMEM((zs * ns // 4, 4 * rows_own), BF),
             pltpu.VMEM((zs, 1, LANES), jnp.int32),
             pltpu.VMEM((1, LANES), jnp.int32),
             pltpu.VMEM((zs, n_c, LANES), F32),
@@ -516,13 +632,15 @@
             pltpu.VMEM((zs, n_c, LANES), BF),
             pltpu.VMEM((n_c, LANES), F32),
             pltpu.VMEM((1, width), F32),
-            pltpu.VMEM((ns // m, tok_len, group_w + LANES), BF),
-            pltpu.VMEM((ns, tok_len, group_w + LANES), BF),
-            pltpu.VMEM((nx, 1, group_w), F32),
+            pltpu.VMEM((ny, tok_len, nx * slice_w), F32),
+            pltpu.VMEM((nx, tok_len, ny * slice_w), F32),
+            pltpu.VMEM((nx * ny, tok_len, group_w), BF),
+            pltpu.VMEM((2, nx * ny, tok_len, group_w), BF),
+            pltpu.VMEM((nx * ny, 1, group_w), F32),
             pltpu.VMEM((ns, 1, group_w), F32),
+            pltpu.VMEM((kv_w, slice_w), BF),
             pltpu.VMEM((group_w, block), BF),
             pltpu.VMEM((m, 2 * buckets, LANES), BF),
-            pltpu.VMEM((2 * buckets, group_w), BF),
             pltpu.VMEM((ns, tok_len, block), F32),
             pltpu.VMEM((ns, tok_len, block), F32),
             pltpu.VMEM((ns, 2, block), F32),
@@ -538,11 +656,12 @@
             pltpu.VMEM((slot, LANES), BF),
             pltpu.VMEM((ns, slot, LANES), BF),
             pltpu.VMEM((ns, slot, LANES), F32),
-            pltpu.VMEM((ns, LANES), BF),
-            pltpu.VMEM((zs, ns, LANES), BF),
-            pltpu.SemaphoreType.DMA((6,)),
-            pltpu.SemaphoreType.DMA((10,)),
-            pltpu.SemaphoreType.DMA((10,)),
+            pltpu.VMEM((ns * 3 // 4, LANES), F32),
+            pltpu.VMEM((ns * 3 // 4, LANES), BF),
+            pltpu.VMEM((zs, ns * 3 // 4, LANES), BF),
+            pltpu.SemaphoreType.DMA((11,)),
+            pltpu.SemaphoreType.DMA((13,)),
+            pltpu.SemaphoreType.DMA((13,)),
         ],
         compiler_params=pltpu.CompilerParams(collective_id=0, has_side_effects=True),
     )(

time: 69 us -> 61.4 us (0.89)
  Pallas kernels: 65.3 us -> 57.8 us
    pallas_call x1, Pallas kernels: 65.3 us -> 57.8 us  [shards(): pl.pallas_call(functools.partial(step_kernel, (zs, nx, ny)), out_shape=ja...]
where the time goes in v3:
time: 61.4 us; the launch traced here: 61.2 us
  Pallas kernels  57.8 us (94%)
  between operations  1.95 us (3%)
  local copies, waits for them, and re-layouts  1.54 us (3%)
    pallas_call x1, Pallas kernels, shards(): pl.pallas_call(functools.partial(step_kernel, (zs, nx, ny)), out_shape=ja...  57.8 us
    unnamed x1, local copies, waits for them, and re-layouts  1.54 us

profile of v3, /device:TPU:1, one launch (start us, length us, event | category | flops | bytes accessed | tf_op | source)
XLA Modules:
  0.0 61.2 jit_solution(5607001504349783132)
XLA Ops:
  1.9 57.8 %shard_map.136 = f32[96,256]{1,0:T(8,128)} custom-call(s32[1]{0:T(128)S(6)} %copy.16.ids_s, s32[1]{0:T(128)S(6)} %copy.17.pos_s, s32[1]{0:T(128)S(6)} %copy.18.time_s, bf16[8,3072]{1,0:T(8,128)(2,1)} %bitcast.14, s32[1,256]{1,0:T(1,128)} %bitcast.16, bf16[64,2,96]{2,1,0:T(2,128)(2,1)} %mods_any.1, f32[1,3072]{1,0:T(1,128)} %bitcast.15, f32[1,128]{1,0:T(1,128)} %bitcast.17, ...), custom_call_target="tpu_custom_call" | custom-call | tf_op jit(solution)/shard_map/pallas_call | solution.py:603
  59.7 1.5 %copy.19 = f32[256,96]{0,1:T(8,128)} copy(f32[256,96]{0,1:T(8,128)} %bitcast.13) | data formatting | bytes 196608

commit v4 on v3

--- a/solution.py
+++ b/solution.py
@@ -50,7 +50,10 @@
     k_any,
     v_any,
     g_any,
-    out,
+    g_recv,
+    belongs_a,
+    belongs_b,
+    meta,
     tok,
     counts,
     mods,
@@ -68,8 +71,6 @@
     lab_recv,
     idz_own,
     idz_recv,
-    belongs_a,
-    belongs_b,
     id_buf,
     id_own,
     row32,
@@ -103,7 +104,6 @@
     dkv_wide,
     g32,
     g_own,
-    g_recv,
     load_sem,
     send_sem,
     recv_sem,
@@ -317,15 +317,6 @@
     finish(tok_recv.at[0, pl.ds(0, chips - 1)], 4)
     remote(tok_recv.at[my_c], tok_recv.at[my_c], 12, (z, f + 1 - 2 * my_c)).start()
 
-    lax.fori_loop(half, heads, image_head, 0)
-
-    table_f = table[...].astype(F32)
-    t_centre = jnp.mean(table_f, -1, keepdims=True)
-    t_spread = jnp.mean((table_f - t_centre) ** 2, -1, keepdims=True)
-    t_rstd = lax.rsqrt(t_spread + EPSILON)
-    diag = iota((rows_own, rows_own), 0) == iota((rows_own, rows_own), 1)
-    own_scale = jnp.sum(jnp.where(diag, t_rstd, 0.0), 0, keepdims=True) / counts[...].astype(F32)
-
     finish(mod_recv.at[pl.ds(0, m - 1)], 2)
     lane_row = iota((LANES, group_w), 0)
     lane_col = iota((LANES, group_w), 1)
@@ -355,6 +346,15 @@
     part_recv[from_me] = part[me]
     for peer, slot in plane:
         remote(part.at[slot], part_recv.at[from_me], 5, (z, peer)).start()
+
+    lax.fori_loop(half, heads, image_head, 0)
+
+    table_f = table[...].astype(F32)
+    t_centre = jnp.mean(table_f, -1, keepdims=True)
+    t_spread = jnp.mean((table_f - t_centre) ** 2, -1, keepdims=True)
+    t_rstd = lax.rsqrt(t_spread + EPSILON)
+    diag = iota((rows_own, rows_own), 0) == iota((rows_own, rows_own), 1)
+    meta[...] = jnp.sum(jnp.where(diag, t_rstd, 0.0), 0, keepdims=True) / counts[...].astype(F32)
 
     finish(row_recv.at[pl.ds(0, zs - 1)], 3)
     concept = jnp.sum(row_recv[...].astype(F32), 0)
@@ -399,11 +399,11 @@
     concept_own = jnp.dot(concepts.astype(BF), own_place, preferred_element_type=F32)
 
     finish(idz_recv.at[pl.ds(0, zs - 1)], 11)
+    half_n, quarter = ns // 2, ns // 4
     id_cols = jnp.sum(
         jnp.where(sample_diag.reshape(1, ns, LANES), idz_recv[...], 0.0), -1, keepdims=True
     ).astype(jnp.int32)
     belongs = (iota((zs, ns, rows_own), 2) + z * rows_own == id_cols).astype(F32)
-    half_n, quarter = ns // 2, ns // 4
     for c in range(2):
         belongs_a[:, c * rows_own : (c + 1) * rows_own] = (
             belongs[:, c * half_n : (c + 1) * half_n, :].reshape(zs * half_n, rows_own).astype(BF)
@@ -528,26 +528,6 @@
     for peer in line:
         remote(g_own, g_recv.at[z], 8, (peer, f)).start()
     finish(g_recv.at[pl.ds(0, zs - 1)], 8)
-    wide = g_recv[...].astype(F32)
-    sum_a = lax.dot_general(
-        wide[:, :half_n, :].reshape(zs * half_n, LANES).astype(BF),
-        belongs_a[...],
-        TN_DIMS,
-        preferred_element_type=F32,
-    )
-    sum_b = lax.dot_general(
-        wide[:, half_n:, :].reshape(zs * quarter, LANES).astype(BF),
-        belongs_b[...],
-        TN_DIMS,
-        preferred_element_type=F32,
-    )
-    top_rows = sum_a[:64, :rows_own] + sum_a[64:, rows_own:]
-    low_rows = sum_b[:32, :rows_own]
-    for c in range(1, 4):
-        low_rows += sum_b[c * 32 : c * 32 + 32, c * rows_own : (c + 1) * rows_own]
-    out[:64, :] = top_rows * own_scale
-    out[64:, :] = low_rows * own_scale
-
     drain(id_buf.at[pl.ds(0, zs - 1)], 0)
     drain(w_recv.at[pl.ds(0, (m - 1) * slice_w)], 1)
     drain(mod_recv.at[pl.ds(0, m - 1)], 2)
@@ -561,6 +541,34 @@
     drain(c_recv.at[pl.ds(0, ns - 1)], 9)
     drain(lab_recv.at[pl.ds(0, ns - 1)], 10)
     drain(idz_recv.at[pl.ds(0, zs - 1)], 11)
+
+
+def owner_kernel(g_recv, belongs_a, belongs_b, meta, out):
+    zs = g_recv.shape[0]
+    half_n = g_recv.shape[1] * 2 // 3
+    quarter = half_n // 2
+    rows_own = meta.shape[1]
+    own_scale = meta[...]
+
+    wide = g_recv[...].astype(F32)
+    sum_a = lax.dot_general(
+        wide[:, :half_n, :].reshape(zs * half_n, LANES).astype(BF),
+        belongs_a[...],
+        TN_DIMS,
+        preferred_element_type=F32,
+    )
+    sum_b = lax.dot_general(
+        wide[:, half_n:, :].reshape(zs * quarter, LANES).astype(BF),
+        belongs_b[...],
+        TN_DIMS,
+        preferred_element_type=F32,
+    )
+    top_rows = sum_a[:64, :rows_own] + sum_a[64:, rows_own:]
+    low_rows = sum_b[:32, :rows_own]
+    for c in range(1, 4):
+        low_rows += sum_b[c * 32 : c * 32 + 32, c * rows_own : (c + 1) * rows_own]
+    out[:64, :] = top_rows * own_scale
+    out[64:, :] = low_rows * own_scale
 
 
 def shards(
@@ -600,11 +608,16 @@
     hb = pl.BlockSpec(memory_space=pl.ANY)
     image = pltpu.VMEM((n_img, head_w), BF)
     stat = pltpu.VMEM((heads, 1, n_img), F32)
-    grad_t = pl.pallas_call(
+    outs = pl.pallas_call(
         functools.partial(step_kernel, (zs, nx, ny)),
-        out_shape=jax.ShapeDtypeStruct((slice_w, rows_own), F32),
+        out_shape=(
+            pltpu.VMEM((zs, ns * 3 // 4, LANES), BF),
+            pltpu.VMEM((zs * ns // 2, 2 * rows_own), BF),
+            pltpu.VMEM((zs * ns // 4, 4 * rows_own), BF),
+            pltpu.VMEM((1, rows_own), F32),
+        ),
         in_specs=[sm] * 3 + [hb] * 11,
-        out_specs=vm,
+        out_specs=(vm,) * 4,
         scratch_shapes=[
             pltpu.VMEM((tok_len, width), BF),
             pltpu.VMEM((1, rows_own), jnp.int32),
@@ -623,8 +636,6 @@
             pltpu.VMEM((ns, 1, LANES), F32),
             pltpu.VMEM((1, LANES), F32),
             pltpu.VMEM((zs, 1, LANES), F32),
-            pltpu.VMEM((zs * ns // 2, 2 * rows_own), BF),
-            pltpu.VMEM((zs * ns // 4, 4 * rows_own), BF),
             pltpu.VMEM((zs, 1, LANES), jnp.int32),
             pltpu.VMEM((1, LANES), jnp.int32),
             pltpu.VMEM((zs, n_c, LANES), F32),
@@ -658,7 +669,6 @@
             pltpu.VMEM((ns, slot, LANES), F32),
             pltpu.VMEM((ns * 3 // 4, LANES), F32),
             pltpu.VMEM((ns * 3 // 4, LANES), BF),
-            pltpu.VMEM((zs, ns * 3 // 4, LANES), BF),
             pltpu.SemaphoreType.DMA((11,)),
             pltpu.SemaphoreType.DMA((13,)),
             pltpu.SemaphoreType.DMA((13,)),
@@ -680,6 +690,12 @@
         img_value[0],
         out_grad[0],
     )
+    grad_t = pl.pallas_call(
+        owner_kernel,
+        out_shape=jax.ShapeDtypeStruct((slice_w, rows_own), F32),
+        in_specs=[vm] * 4,
+        out_specs=vm,
+    )(*(pltpu.with_memory_space_constraint(o, pltpu.VMEM) for o in outs))
     return grad_t.T
 
 

time: 61.4 us -> 60.2 us (0.980)
  local copies, waits for them, and re-layouts: 1.54 us -> 0 us
    unnamed x1 -> x0, local copies, waits for them, and re-layouts: 1.54 us -> none
    pallas_call x1 -> x2, Pallas kernels: 57.8 us -> 58.2 us  [the longest x1 57.2 us: shards(): pl.pallas_call(functools.partial(step_kernel, (zs, nx, ny)), out_shape=(p...]
where the time goes in v4:
time: 60.2 us; the launch traced here: 60.1 us
  Pallas kernels  58.2 us (97%)
  between operations  1.95 us (3%)
    pallas_call x1, Pallas kernels, shards(): pl.pallas_call(functools.partial(step_kernel, (zs, nx, ny)), out_shape=(p...  57.2 us

profile of v4, /device:TPU:1, one launch (start us, length us, event | category | flops | bytes accessed | tf_op | source)
XLA Modules:
  0.0 60.1 jit_solution(11438299774174636599)
XLA Ops:
  1.9 57.2 %shard_map.136 = (bf16[16,24,128]{2,1,0:T(8,128)(2,1)S(1)}, bf16[256,512]{1,0:T(8,128)(2,1)S(1)}, bf16[128,1024]{1,0:T(8,128)(2,1)S(1)}, f32[1,256]{1,0:T(1,128)S(1)}) custom-call(s32[1]{0:T(128)S(6)} %copy.15.ids_s, s32[1]{0:T(128)S(6)} %copy.16.pos_s, s32[1]{0:T(128)S(6)} %copy.17.time_s, bf16[8,3072]{1,0:T(8,128)(2,1)} %bitcast.13, s32[1,256]{1,0:T(1,128)} %bitcast.15, ...), custom_call_target="tpu_custom_call" | custom-call | tf_op jit(solution)/shard_map/pallas_call | solution.py:611
  59.2 0.9 %shard_map.137 = f32[96,256]{1,0:T(8,128)} custom-call(bf16[16,24,128]{2,1,0:T(8,128)(2,1)S(1)} %get-tuple-element.9.g_recv, bf16[256,512]{1,0:T(8,128)(2,1)S(1)} %get-tuple-element.10.belongs_a, bf16[128,1024]{1,0:T(8,128)(2,1)S(1)} %get-tuple-element.11.belongs_b, f32[1,256]{1,0:T(1,128)S(1)} %get-tuple-element.12.meta), custom_call_target="tpu_custom_call" | custom-call | tf_op jit(solution)/shard_map/pallas_call | solution.py:693

commit v5 on v4

--- a/solution.py
+++ b/solution.py
@@ -95,11 +95,16 @@
     m_img,
     l_img,
     d_img,
+    m_rest,
+    l_rest,
+    d_rest,
     dkv32,
     raw32,
     s1_32,
     s2_32,
     dkv_own,
+    mean_own,
+    mean_recv,
     dkv_recv,
     dkv_wide,
     g32,
@@ -289,8 +294,16 @@
         d_img[h] = jnp.sum(raised.astype(BF).astype(F32) * grads, 0, keepdims=True)
         return c
 
-    half = heads // 2
+    half = heads // 4
     lax.fori_loop(0, half, image_head, 0)
+
+    table_f = table[...].astype(F32)
+    t_centre = jnp.mean(table_f, -1, keepdims=True)
+    t_spread = jnp.mean((table_f - t_centre) ** 2, -1, keepdims=True)
+    t_rstd = lax.rsqrt(t_spread + EPSILON)
+    table[...] = ((table_f - t_centre) * t_rstd).astype(BF)
+    diag = iota((rows_own, rows_own), 0) == iota((rows_own, rows_own), 1)
+    meta[...] = jnp.sum(jnp.where(diag, t_rstd, 0.0), 0, keepdims=True) / counts[...].astype(F32)
 
     finish(id_buf.at[pl.ds(0, zs - 1)], 0)
     wanted = id_buf[:, 0, :][:, :1]
@@ -349,19 +362,9 @@
 
     lax.fori_loop(half, heads, image_head, 0)
 
-    table_f = table[...].astype(F32)
-    t_centre = jnp.mean(table_f, -1, keepdims=True)
-    t_spread = jnp.mean((table_f - t_centre) ** 2, -1, keepdims=True)
-    t_rstd = lax.rsqrt(t_spread + EPSILON)
-    diag = iota((rows_own, rows_own), 0) == iota((rows_own, rows_own), 1)
-    meta[...] = jnp.sum(jnp.where(diag, t_rstd, 0.0), 0, keepdims=True) / counts[...].astype(F32)
-
     finish(row_recv.at[pl.ds(0, zs - 1)], 3)
     concept = jnp.sum(row_recv[...].astype(F32), 0)
-    c_mean = jnp.sum(jnp.sum(concept, -1, keepdims=True), 0, keepdims=True) / width
-    c_diff = concept - c_mean
-    c_var = jnp.sum(jnp.sum(c_diff * c_diff, -1, keepdims=True), 0, keepdims=True) / width
-    c32[...] = (c_diff * lax.rsqrt(c_var + EPSILON)).astype(BF).astype(F32)
+    c32[...] = concept
     for c in range(width // LANES):
         c_row[:, c * LANES : (c + 1) * LANES] = c32[c : c + 1, :]
     for a in range(nx):
@@ -420,30 +423,23 @@
         w_t[lanes, :] = weight[:, lanes].astype(F32).T.astype(BF)
 
     finish(part_recv.at[pl.ds(0, ns - 1)], 5)
-    finish(late_recv.at[pl.ds(0, ns - 1)], 6)
     per = block // LANES
     pos_f = at_pos.astype(F32)
     for c in range(m):
         total = part_recv[c]
-        extras = late_recv[c]
         for a in range(1, groups):
             total += part_recv[a * m + c]
-            extras += late_recv[a * m + c]
         first = jnp.sum(total * pos_f, 0, keepdims=True)
-        kv[:, c * block : (c + 1) * block] = jnp.where(at_pos, extras[0:1, :], total)
+        kv[:, c * block : (c + 1) * block] = total + bias[:, c * block : (c + 1) * block]
         for b in range(per):
             s1_32[c * per + b : c * per + b + 1, :] = first[:, b * LANES : (b + 1) * LANES]
-            s2_32[c * per + b : c * per + b + 1, :] = extras[1:2, b * LANES : (b + 1) * LANES]
-
-    kv_all = kv[...] + bias[...]
+    kv_all = kv[...]
     gains = gain[...]
-    raw_row = jnp.sum(kv_all[:, :head_w] * pos_f, 0, keepdims=True)
     key_parts = []
     for h in range(heads):
         raw = kv_all[:, h * LANES : (h + 1) * LANES]
         inv = lax.rsqrt(jnp.mean(raw * raw, -1, keepdims=True) + EPSILON)
         key_parts.append((raw * inv * gains).astype(BF).astype(F32))
-        raw32[h : h + 1, :] = raw_row[:, h * LANES : (h + 1) * LANES]
     key_txt = jnp.concatenate(key_parts, 1)
     val_txt = kv_all[:, head_w:].astype(BF).astype(F32)
     own_head = iota((heads * tok_len, head_w), 0) // tok_len == iota(
@@ -457,19 +453,44 @@
     g_txt = lax.dot_general(val_diag, g[...], NT_DIMS, preferred_element_type=F32).reshape(
         heads, tok_len, n_img
     )
+    other = iota((1, tok_len, 1), 1) != own_pos
     top_img = m_img[...]
-    top = jnp.maximum(top_img, jnp.max(s_txt, 1, keepdims=True))
-    raised = jnp.exp(s_txt - top)
+    top = jnp.maximum(top_img, jnp.max(jnp.where(other, s_txt, -3e38), 1, keepdims=True))
+    raised = jnp.where(other, jnp.exp(jnp.where(other, s_txt, top) - top), 0.0)
     alpha = jnp.exp(top_img - top)
-    denom = alpha * l_img[...] + jnp.sum(raised, 1, keepdims=True)
-    probs = raised / denom
-    delta = alpha * d_img[...] / denom + jnp.sum(
-        probs.astype(BF).astype(F32) * g_txt, 1, keepdims=True
-    )
-    pos_3 = (iota((1, tok_len, 1), 1) == own_pos).astype(F32)
-    p_pos = jnp.sum(probs * pos_3, 1)
-    g_pos = jnp.sum(g_txt * pos_3, 1)
-    d_score = p_pos * (g_pos - delta[:, 0, :]) * inv_root
+    m_rest[...] = top[:, 0, :]
+    l_rest[...] = (alpha * l_img[...] + jnp.sum(raised, 1, keepdims=True))[:, 0, :]
+    d_rest[...] = (
+        alpha * d_img[...] + jnp.sum(raised.astype(BF).astype(F32) * g_txt, 1, keepdims=True)
+    )[:, 0, :]
+
+    finish(late_recv.at[pl.ds(0, ns - 1)], 6)
+    for c in range(m):
+        extras = late_recv[c]
+        for a in range(1, groups):
+            extras += late_recv[a * m + c]
+        raw_row = extras[0:1, :] + bias[:, c * block : (c + 1) * block]
+        for b in range(per):
+            lanes = slice(b * LANES, (b + 1) * LANES)
+            raw32[c * per + b : c * per + b + 1, :] = raw_row[:, lanes]
+            s2_32[c * per + b : c * per + b + 1, :] = extras[1:2, lanes]
+    raw_pos = raw32[:heads, :]
+    inv_pos = lax.rsqrt(jnp.mean(raw_pos * raw_pos, -1, keepdims=True) + EPSILON)
+    key_pos = (raw_pos * inv_pos * gains).astype(BF).astype(F32)
+    val_pos = raw32[heads:, :].astype(BF).astype(F32)
+    own_lane = iota((heads, head_w), 0) == iota((heads, head_w), 1) // LANES
+    key_diag = jnp.where(own_lane, jnp.concatenate([key_pos] * heads, 1), 0.0).astype(BF)
+    val_diag = jnp.where(own_lane, jnp.concatenate([val_pos] * heads, 1), 0.0).astype(BF)
+    s_pos = lax.dot_general(key_diag, q[...], NT_DIMS, preferred_element_type=F32) * inv_root
+    g_pos = lax.dot_general(val_diag, g[...], NT_DIMS, preferred_element_type=F32)
+    top_rest = m_rest[...]
+    top = jnp.maximum(top_rest, s_pos)
+    raised = jnp.exp(s_pos - top)
+    alpha = jnp.exp(top_rest - top)
+    denom = alpha * l_rest[...] + raised
+    p_pos = raised / denom
+    delta = alpha * d_rest[...] / denom + p_pos.astype(BF).astype(F32) * g_pos
+    d_score = p_pos * (g_pos - delta) * inv_root
     p_high, p_low = split_two(p_pos)
     d_high, d_low = split_two(d_score)
     d_val = jnp.dot(
@@ -484,28 +505,23 @@
     )
     d_val = d_val[:heads] + d_val[heads:]
     d_key = d_key[:heads] + d_key[heads:]
-    dkv32[...] = jnp.zeros(dkv32.shape, F32)
     for h in range(heads):
         dkv32[h : h + 1, :] = d_key[h : h + 1, h * LANES : (h + 1) * LANES]
         dkv32[heads + h : heads + h + 1, :] = d_val[h : h + 1, h * LANES : (h + 1) * LANES]
-    raw_pos = raw32[...]
-    inv_pos = lax.rsqrt(jnp.mean(raw_pos * raw_pos, -1, keepdims=True) + EPSILON)
     n_pos = raw_pos * inv_pos
     d_norm = dkv32[:heads, :] * gains
     dkv32[:heads, :] = inv_pos * (d_norm - n_pos * jnp.mean(d_norm * n_pos, -1, keepdims=True))
-    dkv_rows = dkv32[: 2 * heads, :].astype(BF).astype(F32)
-    mean_1 = jnp.sum(jnp.sum(dkv_rows * s1_32[...], -1, keepdims=True), 0, keepdims=True) / width
-    mean_2 = jnp.sum(jnp.sum(dkv_rows * s2_32[...], -1, keepdims=True), 0, keepdims=True) / width
-    for c, value in enumerate((mean_1, mean_2)):
-        high, low = split_two(value)
-        at = 2 * heads + 2 * c
-        dkv32[at : at + 1, :] = jnp.broadcast_to(high.astype(F32), (1, LANES))
-        dkv32[at + 1 : at + 2, :] = jnp.broadcast_to(low.astype(F32), (1, LANES))
     dkv_own[...] = dkv32[...].astype(BF)
     dkv_recv[me] = dkv_own[...]
 
+    dkv_rows = dkv_own[...].astype(F32)
+    mean_own[0:1, :] = jnp.sum(dkv_rows * s1_32[...], 0, keepdims=True)
+    mean_own[1:2, :] = jnp.sum(dkv_rows * s2_32[...], 0, keepdims=True)
+    mean_recv[me] = mean_own[...]
     for peer, _ in plane:
+        remote(mean_own, mean_recv.at[me], 13, (z, peer)).start()
         remote(dkv_own, dkv_recv.at[me], 7, (z, peer)).start()
+    finish(mean_recv.at[pl.ds(0, ns - 1)], 13)
     finish(dkv_recv.at[pl.ds(0, ns - 1)], 7)
     dkv_wide[...] = dkv_recv[...].astype(F32)
     grads = jnp.zeros((ns, slice_w), F32)
@@ -514,9 +530,8 @@
         grads += jnp.dot(
             both, w_t[c * LANES : (c + 2) * LANES, :], preferred_element_type=F32
         )
-    at = 2 * heads
-    mean_1 = (dkv_wide[:, at, :] + dkv_wide[:, at + 1, :])[:, :slice_w]
-    mean_2 = (dkv_wide[:, at + 2, :] + dkv_wide[:, at + 3, :])[:, :slice_w]
+    mean_1 = jnp.sum(mean_recv[:, 0, :], -1, keepdims=True) / width
+    mean_2 = jnp.sum(mean_recv[:, 1, :], -1, keepdims=True) / width
     row_grad = grads * scale_own[:, :slice_w] - mean_1 - concept_own[:, :slice_w] * mean_2
     for c in range(2):
         g32[:half_n, c * 64 : c * 64 + 64] = row_grad[c * half_n : (c + 1) * half_n, :64]
@@ -541,6 +556,7 @@
     drain(c_recv.at[pl.ds(0, ns - 1)], 9)
     drain(lab_recv.at[pl.ds(0, ns - 1)], 10)
     drain(idz_recv.at[pl.ds(0, zs - 1)], 11)
+    drain(mean_recv.at[pl.ds(0, ns - 1)], 13)
 
 
 def owner_kernel(g_recv, belongs_a, belongs_b, meta, out):
@@ -601,7 +617,7 @@
     block = kv_w // m
     group_w = slice_w * m
     n_c = width // LANES
-    slot = (2 * heads + 4 + 15) // 16 * 16
+    slot = 2 * heads
 
     vm = pl.BlockSpec(memory_space=pltpu.VMEM)
     sm = pl.BlockSpec(memory_space=pltpu.SMEM)
@@ -660,18 +676,23 @@
             stat,
             stat,
             stat,
+            pltpu.VMEM((heads, n_img), F32),
+            pltpu.VMEM((heads, n_img), F32),
+            pltpu.VMEM((heads, n_img), F32),
             pltpu.VMEM((slot, LANES), F32),
-            pltpu.VMEM((heads, LANES), F32),
+            pltpu.VMEM((2 * heads, LANES), F32),
             pltpu.VMEM((2 * heads, LANES), F32),
             pltpu.VMEM((2 * heads, LANES), F32),
             pltpu.VMEM((slot, LANES), BF),
+            pltpu.VMEM((2, LANES), F32),
+            pltpu.VMEM((ns, 2, LANES), F32),
             pltpu.VMEM((ns, slot, LANES), BF),
             pltpu.VMEM((ns, slot, LANES), F32),
             pltpu.VMEM((ns * 3 // 4, LANES), F32),
             pltpu.VMEM((ns * 3 // 4, LANES), BF),
             pltpu.SemaphoreType.DMA((11,)),
-            pltpu.SemaphoreType.DMA((13,)),
-            pltpu.SemaphoreType.DMA((13,)),
+            pltpu.SemaphoreType.DMA((14,)),
+            pltpu.SemaphoreType.DMA((14,)),
         ],
         compiler_params=pltpu.CompilerParams(collective_id=0, has_side_effects=True),
     )(

time: 60.2 us -> 59.5 us (0.988)
  Pallas kernels: 58.2 us -> 57.4 us
    pallas_call x1, Pallas kernels: 57.2 us -> 56.5 us  [shards(): pl.pallas_call(functools.partial(step_kernel, (zs, nx, ny)), out_shape=(p...]
where the time goes in v5:
time: 59.5 us; the launch traced here: 59.3 us
  Pallas kernels  57.4 us (96%)
  between operations  1.95 us (3%)
    pallas_call x1, Pallas kernels, shards(): pl.pallas_call(functools.partial(step_kernel, (zs, nx, ny)), out_shape=(p...  56.5 us

profile of v5, /device:TPU:1, one launch (start us, length us, event | category | flops | bytes accessed | tf_op | source)
XLA Modules:
  0.0 59.3 jit_solution(12263197086511528792)
XLA Ops:
  1.9 56.5 %shard_map.136 = (bf16[16,24,128]{2,1,0:T(8,128)(2,1)S(1)}, bf16[256,512]{1,0:T(8,128)(2,1)S(1)}, bf16[128,1024]{1,0:T(8,128)(2,1)S(1)}, f32[1,256]{1,0:T(1,128)S(1)}) custom-call(s32[1]{0:T(128)S(6)} %copy.15.ids_s, s32[1]{0:T(128)S(6)} %copy.16.pos_s, s32[1]{0:T(128)S(6)} %copy.17.time_s, bf16[8,3072]{1,0:T(8,128)(2,1)} %bitcast.13, s32[1,256]{1,0:T(1,128)} %bitcast.15, ...), custom_call_target="tpu_custom_call" | custom-call | tf_op jit(solution)/shard_map/pallas_call | solution.py:627
  58.4 0.9 %shard_map.137 = f32[96,256]{1,0:T(8,128)} custom-call(bf16[16,24,128]{2,1,0:T(8,128)(2,1)S(1)} %get-tuple-element.9.g_recv, bf16[256,512]{1,0:T(8,128)(2,1)S(1)} %get-tuple-element.10.belongs_a, bf16[128,1024]{1,0:T(8,128)(2,1)S(1)} %get-tuple-element.11.belongs_b, f32[1,256]{1,0:T(1,128)S(1)} %get-tuple-element.12.meta), custom_call_target="tpu_custom_call" | custom-call | tf_op jit(solution)/shard_map/pallas_call | solution.py:714

commit v6 on v5

--- a/solution.py
+++ b/solution.py
@@ -155,12 +155,15 @@
     own_slot = my_c * nx + ring
     own_block = lax.rem(my_x + my_y, ny) * 2 + my_c
     mates = []
+    same_ring = []
     for b, c in sorted(
         ((b, c) for b in range(ny) for c in range(2)), key=lambda bc: -min(bc[0], ny - bc[0])
     ):
         if b or c:
             mate_x = lax.rem(my_x + b * (1 - my_c), nx)
             mate_y = lax.rem(my_y + b * my_c, ny)
+            if c == 0:
+                same_ring.append((mate_x * ny + mate_y) * 2 + my_c)
             mates.append(
                 (
                     (mate_x * ny + mate_y) * 2 + c_at[c],
@@ -263,10 +266,7 @@
     for peer, _ in plane:
         remote(lab_own, lab_recv.at[me], 10, (z, peer)).start()
 
-    for peer, chip in same_core:
-        remote(tok_msg.at[chip], tok_recv.at[my_c, me_chip], 4, (z, peer)).start()
-
-    for peer, _ in mates:
+    for peer in same_ring:
         remote(modp, mod_recv.at[own_slot], 2, (z, peer)).start()
 
     for peer, theirs in mates:
@@ -276,6 +276,9 @@
             1,
             (z, peer),
         ).start()
+
+    for peer, chip in same_core:
+        remote(tok_msg.at[chip], tok_recv.at[my_c, me_chip], 4, (z, peer)).start()
 
     for copy in loads[3:]:
         copy.wait()
@@ -327,10 +330,14 @@
     for peer in line:
         remote(idz_own, idz_recv.at[z], 11, (peer, f)).start()
 
+    ring_slots = mod_recv.at[pl.ds(my_c * nx, nx)]
+    finish(mod_recv.at[pl.ds(0, nx - 1)], 2)
+    remote(ring_slots, ring_slots, 14, (z, f + 1 - 2 * my_c)).start()
+
     finish(tok_recv.at[0, pl.ds(0, chips - 1)], 4)
     remote(tok_recv.at[my_c], tok_recv.at[my_c], 12, (z, f + 1 - 2 * my_c)).start()
 
-    finish(mod_recv.at[pl.ds(0, m - 1)], 2)
+    finish(mod_recv.at[pl.ds(0, nx)], 14)
     lane_row = iota((LANES, group_w), 0)
     lane_col = iota((LANES, group_w), 1)
     mod_sum = jnp.zeros((2 * buckets, group_w), F32)
@@ -545,7 +552,8 @@
     finish(g_recv.at[pl.ds(0, zs - 1)], 8)
     drain(id_buf.at[pl.ds(0, zs - 1)], 0)
     drain(w_recv.at[pl.ds(0, (m - 1) * slice_w)], 1)
-    drain(mod_recv.at[pl.ds(0, m - 1)], 2)
+    drain(mod_recv.at[pl.ds(0, nx - 1)], 2)
+    drain(mod_recv.at[pl.ds(0, nx)], 14)
     drain(row_recv.at[pl.ds(0, zs - 1)], 3)
     drain(tok_recv.at[0, pl.ds(0, chips - 1)], 4)
     drain(tok_recv.at[0], 12)
@@ -691,8 +699,8 @@
             pltpu.VMEM((ns * 3 // 4, LANES), F32),
             pltpu.VMEM((ns * 3 // 4, LANES), BF),
             pltpu.SemaphoreType.DMA((11,)),
-            pltpu.SemaphoreType.DMA((14,)),
-            pltpu.SemaphoreType.DMA((14,)),
+            pltpu.SemaphoreType.DMA((15,)),
+            pltpu.SemaphoreType.DMA((15,)),
         ],
         compiler_params=pltpu.CompilerParams(collective_id=0, has_side_effects=True),
     )(

time: 59.5 us -> 59.5 us (level)
  no operation moved by 1% of the time
where the time goes in v6:
time: 59.5 us; the launch traced here: 59.4 us
  Pallas kernels  57.4 us (96%)
  between operations  1.95 us (3%)
    pallas_call x1, Pallas kernels, shards(): pl.pallas_call(functools.partial(step_kernel, (zs, nx, ny)), out_shape=(p...  56.5 us

profile of v6, /device:TPU:1, one launch (start us, length us, event | category | flops | bytes accessed | tf_op | source)
XLA Modules:
  0.0 59.4 jit_solution(5576332881294436720)
XLA Ops:
  1.9 56.5 %shard_map.136 = (bf16[16,24,128]{2,1,0:T(8,128)(2,1)S(1)}, bf16[256,512]{1,0:T(8,128)(2,1)S(1)}, bf16[128,1024]{1,0:T(8,128)(2,1)S(1)}, f32[1,256]{1,0:T(1,128)S(1)}) custom-call(s32[1]{0:T(128)S(6)} %copy.15.ids_s, s32[1]{0:T(128)S(6)} %copy.16.pos_s, s32[1]{0:T(128)S(6)} %copy.17.time_s, bf16[8,3072]{1,0:T(8,128)(2,1)} %bitcast.13, s32[1,256]{1,0:T(1,128)} %bitcast.15, ...), custom_call_target="tpu_custom_call" | custom-call | tf_op jit(solution)/shard_map/pallas_call | solution.py:635
  58.4 0.9 %shard_map.137 = f32[96,256]{1,0:T(8,128)} custom-call(bf16[16,24,128]{2,1,0:T(8,128)(2,1)S(1)} %get-tuple-element.9.g_recv, bf16[256,512]{1,0:T(8,128)(2,1)S(1)} %get-tuple-element.10.belongs_a, bf16[128,1024]{1,0:T(8,128)(2,1)S(1)} %get-tuple-element.11.belongs_b, f32[1,256]{1,0:T(1,128)S(1)} %get-tuple-element.12.meta), custom_call_target="tpu_custom_call" | custom-call | tf_op jit(solution)/shard_map/pallas_call | solution.py:722
